TPU v7x, 32 devices: a whole 2x2x4 slice. The times are simulated.
32 devices in a mesh: strip: 8 (over y, x, core), view: 4 (over z).
Axes of the slice: x: 2, y: 2, z: 4, core: 2. Of those that a mesh axis runs over, the one named last changes fastest.
Arguments:
- images: bfloat16 [4, 1024, 640], P('view', 'strip'), may hold values from -6 to 6
- offsets: int32 [4, 8], P(None, 'strip'), may hold values from 0 to 376
- pair_step: int32 [8], P('strip'), may hold values from 1 to 3
- row_map: int32 [1024], replicated, may hold values from 0 to 1023, as said below
Outputs:
- cost_volume: bfloat16 [4, 128, 1024, 128], P('view', None, 'strip')
Inputs may be any that keep to these rules, and one draw needn't show every extreme that they name: `row_map`: A permutation of the 1024 rows. Of the 128 entries in each aligned block of 128 tile rows, exactly 16 fall in each aligned block of 128 strip rows.
All inputs are finite; a program needn't handle non-finite values.
Results may differ from a plain program's by a relative error of at most 0.001.
Values may be sent and summed in bfloat16 or wider, within the bound.
No kernel may reach another device: no remote copies, remote signals or barrier semaphores. Data moves between devices by JAX's collectives and lax.ppermute only.
A program may use at most 64 MiB of HBM per device.

v0:
```python
import jax
import jax.numpy as jnp
from jax import lax
from jax.sharding import PartitionSpec as P

COLS = 128
DISP = 128
OFF_MAX = 376


EPSILON = 1e-05


def for_sending(value):

    def short(part):
        return part.astype(jnp.bfloat16) if part.dtype == jnp.float32 else part

    return jax.tree.map(short, value)


def passed_along(value, axis, by):
    size = lax.axis_size(axis)
    return lax.ppermute(value, axis, [(i, (i + by) % size) for i in range(size)])


def with_halo(cells, sides, width):
    for axis, dim in sides:
        count = lax.axis_size(axis)
        ends = count - 1
        head = lax.slice_in_dim(cells, 0, width, axis=dim)
        tail = lax.slice_in_dim(cells, cells.shape[dim] - width, cells.shape[dim], axis=dim)
        cells = jnp.concatenate(
            [
                lax.ppermute(tail, axis, [(i, (i + 1) % count) for i in range(ends)]),
                cells,
                lax.ppermute(head, axis, [((i + 1) % count, i) for i in range(ends)]),
            ],
            axis=dim,
        )
    return cells


def box_sum(values):
    out_rows = values.shape[-2] - 8
    out_cols = values.shape[-1] - 8
    row_sums = values[..., 0:out_rows, :]
    for shift_row in range(1, 9):
        row_sums = row_sums + values[..., shift_row : shift_row + out_rows, :]
    box_total = row_sums[..., 0:out_cols]
    for shift_col in range(1, 9):
        box_total = box_total + row_sums[..., shift_col : shift_col + out_cols]
    return box_total


def cost_block(ref_window, mate_window):
    ref_float = ref_window.astype(jnp.float32)
    mate_float = mate_window.astype(jnp.float32)
    rows_out = ref_window.shape[0] - 8
    cols_out = ref_window.shape[1] - 8
    sum_ref = box_sum(ref_float)
    sum_ref_sq = box_sum(ref_float * ref_float)
    mean_ref = sum_ref / 81.0
    var_ref = sum_ref_sq / 81.0 - mean_ref * mean_ref
    mate_box = box_sum(mate_float)
    mate_box_sq = box_sum(mate_float * mate_float)

    def block_step(block_index, volume):
        first_disp = (block_index * 16).astype(jnp.int32)
        starts = [DISP - 1 - within - first_disp for within in range(16)]
        shifted = jnp.stack(
            [lax.dynamic_slice_in_dim(mate_float, begin, cols_out + 8, 1) for begin in starts]
        )
        sum_cross = box_sum(ref_float[None] * shifted)
        sum_mate = jnp.stack(
            [lax.dynamic_slice_in_dim(mate_box, begin, cols_out, 1) for begin in starts]
        )
        sum_mate_sq = jnp.stack(
            [lax.dynamic_slice_in_dim(mate_box_sq, begin, cols_out, 1) for begin in starts]
        )
        mean_mate = sum_mate / 81.0
        var_mate = sum_mate_sq / 81.0 - mean_mate * mean_mate
        covariance = sum_cross / 81.0 - mean_ref * mean_mate
        ncc_score = covariance * lax.rsqrt((var_ref + EPSILON) * (var_mate + EPSILON))
        return lax.dynamic_update_slice_in_dim(
            volume, ncc_score.astype(jnp.bfloat16), first_disp, 0
        )

    empty = jnp.zeros((DISP, rows_out, cols_out), jnp.bfloat16)
    return lax.fori_loop(0, DISP // 16, block_step, empty)


def rotate_by(step_size, view_me, view_count, offsets, span_cols):

    def branch(own_rows):
        receiver = (view_me - step_size) % view_count
        slab = lax.dynamic_slice_in_dim(own_rows, OFF_MAX - offsets[receiver, 0], span_cols, 1)
        return passed_along(for_sending(slab), "view", view_count - step_size).astype(slab.dtype)

    return branch


def shards(images, offsets, pair_step, row_map):
    own_tiles = images[0]
    rows_dev = own_tiles.shape[0]
    width_all = own_tiles.shape[1]
    span_cols = COLS + DISP + 8
    strip_count = lax.axis_size("strip")
    view_count = lax.axis_size("view")
    strip_me = lax.axis_index("strip")
    view_me = lax.axis_index("view")
    per_peer = rows_dev // strip_count
    local_map = lax.dynamic_slice_in_dim(row_map, strip_me * rows_dev, rows_dev)
    targets = local_map // rows_dev
    send_order = jnp.argsort(targets, stable=True)
    outgoing = own_tiles[send_order].reshape(strip_count, per_peer, width_all)
    arrived = lax.all_to_all(outgoing, "strip", split_axis=0, concat_axis=0, tiled=True)
    whole_table = row_map.reshape(strip_count, rows_dev)
    hits = whole_table // rows_dev == strip_me
    column_ids = lax.broadcasted_iota(jnp.int32, whole_table.shape, 1)
    rank_keys = jnp.where(hits, column_ids, column_ids + rows_dev)
    picked = jnp.argsort(rank_keys, axis=1, stable=True)[:, :per_peer]
    slot_ids = jnp.take_along_axis(whole_table % rows_dev, picked, axis=1).reshape(rows_dev)
    inverse = jnp.argsort(slot_ids)
    strip_rows = arrived.reshape(rows_dev, width_all)[inverse]
    bordered = with_halo(strip_rows[None], (("strip", 1),), 4)
    own_rows = bordered[0]
    step_now = pair_step[0] % view_count
    branches = [
        rotate_by(step_size, view_me, view_count, offsets, span_cols)
        for step_size in range(1, view_count)
    ]
    mate_window = lax.switch(step_now - 1, branches, own_rows)
    ref_window = own_rows[:, OFF_MAX + DISP - 1 : OFF_MAX + DISP - 1 + COLS + 8]
    volume = cost_block(ref_window, mate_window)
    return volume[None]


def solution(mesh):
    in_specs = (P("view", "strip", None), P(None, "strip"), P("strip"), P())
    out_specs = P("view", None, "strip", None)
    return jax.shard_map(shards, mesh=mesh, in_specs=in_specs, out_specs=out_specs, check_vma=False)
```

profile of v0, /device:TPU:0, one launch (start us, length us, event | category | flops | bytes accessed | tf_op | source)
XLA Modules:
  0.0 130.3 jit_solution(3409880606353496173)
XLA Ops:
  6.5 1.3 %iota_select_fusion = (s32[8,128]{1,0:T(8,128)}, s32[8,128]{1,0:T(8,128)S(1)}) fusion(s32[1024]{0:T(1024)} %param.12, s32[128]{0:T(128)S(1)} %iota_add_fusion, s32[]{:T(128)S(6)} %axis_index.23), kind=kLoop, calls=%fused_computation.165 | loop fusion | flops 21504 | bytes 12804 | tf_op jit(solution)/shard_map/jit(_where)/select_n | solution.py:121
  7.9 0.6 iota.27
  8.5 0.8 and_select_fusion.1
  9.3 2.5 %sort.51 = (s32[128]{0:T(128)}, s32[128]{0:T(128)S(1)}) sort(s32[128]{0:T(128)S(1)} %and_select_fusion.1, s32[128]{0:T(128)S(1)} %iota.23), dimensions={0}, to_apply=%region_0.1 | sort | flops 896 | bytes 2048 | tf_op jit(solution)/shard_map/jit(argsort)/sort | solution.py:115
  11.8 1.5 %gather_fusion = bf16[128,640]{1,0:T(8,128)(2,1)} fusion(bf16[128,640]{1,0:T(8,128)(2,1)S(1)} %bitcast.239, s32[1024]{0:T(1024)S(1)} %pad_clamp_fusion.1), kind=kCustom, calls=%fused_computation | custom fusion | bytes 328192 | tf_op jit(solution)/shard_map/gather | solution.py:116
  13.3 5.2 %all-to-all-start = ((bf16[8,16,640]{2,1,0:T(8,128)(2,1)}), bf16[8,16,640]{2,1,0:T(8,128)(2,1)S(1)}, u32[]{:S(2)}, u32[]{:S(2)}) async-start(bf16[8,16,640]{2,1,0:T(8,128)(2,1)} %bitcast.55), calls=%async_computation | async-start | bytes 327680 | tf_op jit(solution)/shard_map/all_to_all | solution.py:117
  18.6 0.8 bitcast_or_fusion
  19.4 1.0 gather_fusion.2
  20.6 2.6 %sort.53 = (s32[128]{0:T(128)}, s32[128]{0:T(128)S(1)}) sort(s32[128]{0:T(128)S(1)} %select_n.464, s32[128]{0:T(128)S(1)} %iota.28), dimensions={0}, to_apply=%region_2.3 | sort | flops 896 | bytes 2048 | tf_op jit(solution)/shard_map/jit(argsort)/sort | solution.py:124
  23.2 1.2 all-to-all-done
  24.4 0.9 gather_fusion.1
  25.3 1.5 %collective-permute-start.3 = (bf16[1,4,640]{2,1,0:T(4,128)(2,1)S(1)}, bf16[1,4,640]{2,1,0:T(4,128)(2,1)S(1)}, u32[]{:S(2)}, u32[]{:S(2)}) collective-permute-start(bf16[1,4,640]{2,1,0:T(4,128)(2,1)S(1)} %get-tuple-element.381), channel_id=1, source_target_pairs={{0,4},{4,8},{8,12},{12,16},{16,20},{20,24},{24,28},{1,5},{5,9},{9,... | collective-permute-start | bytes 15368 | tf_op jit(solution)/shard_map/ppermute | solution.py:35
  26.9 1.3 collective-permute-start.4
  28.8 1.8 %collective-permute-done.4 = bf16[1,4,640]{2,1,0:T(4,128)(2,1)S(1)} collective-permute-done((bf16[1,4,640]{2,1,0:T(4,128)(2,1)S(1)}, bf16[1,4,640]{2,1,0:T(4,128)(2,1)S(1)}, u32[]{:S(2)}, u32[]{:S(2)}) %collective-permute-start.4) | collective-permute-done | bytes 5152 | tf_op jit(solution)/shard_map/ppermute | solution.py:37
  30.9 9.4 %conditional.1 = (bf16[136,264]{1,0:T(8,128)(2,1)}) conditional(s32[]{:T(128)} %clamp.3, (s32[]{:T(128)}, s32[4,1]{0,1:T(1,128)S(1)}, bf16[136,640]{1,0:T(8,128)(2,1)S(1)}) %tuple.72, (s32[]{:T(128)}, s32[4,1]{0,1:T(1,128)S(1)}, bf16[136,640]{1,0:T(8,128)(2,1)S(1)}) %tuple.73, (s32[]{:T(128)}, s32[4,1]{0,1:T(1,128)S(1)}, ...), branch_computations={%region_3.4_spmd, %region_4.5_spmd, %region_5.6_spmd} | conditional | flops 19 | bytes 431105 | solution.py:133
  31.0 0.6 fusion.16
  33.6 1.6 %collective-permute-start.2 = (bf16[136,264]{1,0:T(8,128)(2,1)S(1)}, bf16[136,264]{1,0:T(8,128)(2,1)}, u32[]{:S(2)}, u32[]{:S(2)}) collective-permute-start(bf16[136,264]{1,0:T(8,128)(2,1)S(1)} %constant_dynamic-slice_fusion.4), channel_id=1, source_target_pairs={{0,1},{1,2},{2,3},{3,0},{4,5},{5,6},{6,7},{7,4},{8,9},{9,10},{10,1... | collective-permute-start | bytes 215432 | tf_op jit(solution)/shard_map/cond/branch_2_fun/ppermute | solution.py:24
  35.3 5.1 %collective-permute-done.2 = bf16[136,264]{1,0:T(8,128)(2,1)} collective-permute-done((bf16[136,264]{1,0:T(8,128)(2,1)S(1)}, bf16[136,264]{1,0:T(8,128)(2,1)}, u32[]{:S(2)}, u32[]{:S(2)}) %collective-permute-start.2) | collective-permute-done | bytes 71840 | tf_op jit(solution)/shard_map/cond/branch_2_fun/ppermute | solution.py:24
  40.3 0.9 convert_element_type.18
  41.2 0.9 convert_multiply_fusion
  42.2 0.1 slice_add_fusion.16
  42.3 0.1 slice_add_fusion.24
  42.5 0.2 slice_add_fusion.40
  42.7 0.3 fusion.6
  43.0 0.6 slice_add_fusion.32
  43.6 3.1 %broadcast_in_dim.28 = bf16[128,128,128]{2,1,0:T(8,128)(2,1)} broadcast(bf16[]{:T(256)} %constant.462.clone.1), dimensions={} | broadcast | bytes 4194306 | tf_op jit(solution)/shard_map/broadcast_in_dim | solution.py:89
  46.7 76.8 %while.16 = (s32[]{:T(128)}, bf16[128,128,128]{2,1,0:T(8,128)(2,1)}, f32[136,136]{1,0:T(8,128)S(1)}, f32[136,264]{1,0:T(8,128)S(1)}, f32[128,256]{1,0:T(8,128)S(...) while((s32[]{:T(128)}, ...), condition=%wide.region_7.8_spmd, body=%wide.region_6.7_spmd.sunk | while | flops 7537758 | bytes 34621616 | solution.py:90
  50.1 0.1 bitcast_dynamic-update-slice_fusion.36
  50.2 0.1 bitcast_dynamic-update-slice_fusion.37
  50.6 0.1 bitcast_dynamic-update-slice_fusion.40
  50.7 0.1 bitcast_dynamic-update-slice_fusion.41
  50.8 0.1 bitcast_dynamic-update-slice_fusion.42
  51.1 0.1 bitcast_dynamic-update-slice_fusion.45
  51.2 0.1 bitcast_dynamic-update-slice_fusion.46
  51.5 0.2 broadcast_multiply_fusion.3
  51.6 1.6 %slice_add_fusion.81 = f32[16,128,136]{2,1,0:T(8,128)S(1)} fusion(f32[16,136,136]{2,1,0:T(8,128)S(1)} %broadcast_multiply_fusion.3), kind=kLoop, calls=%fused_computation.9.clone.1 | loop fusion | flops 2228224 | bytes 11141120 | tf_op jit(solution)/shard_map/while/body/eval_jaxpr/add | solution.py:49
  53.2 3.0 %fusion.19 = bf16[128,128,128]{2,1,0:T(8,128)(2,1)} fusion(bf16[128,128,128]{2,1,0:T(8,128)(2,1)} %get-tuple-element.499, s32[]{:T(128)S(6)} %select_n.516, f32[16,128,128]{2,1,0:T(8,128)S(1)} %get-tuple-element.442, f32[16,128,128]{2,1,0:T(8,128)S(1)} %get-tuple-element.443, f32[16,128,136]{2,1,0:T(8,128)S(1)} %slice_add_fusion.81, ...), kind=kLoop, calls=%fused_computation.30.clone.1 | loop fusion | flops 4980736 | bytes 12189700 | tf_op jit(solution)/shard_map/while/body/eval_jaxpr/dynamic_update_slice | solution.py:85
  59.4 0.1 bitcast_dynamic-update-slice_fusion.33
  59.5 0.1 bitcast_dynamic-update-slice_fusion.34
  59.8 0.1 bitcast_dynamic-update-slice_fusion.37
  59.9 0.1 bitcast_dynamic-update-slice_fusion.38
  60.4 0.1 bitcast_dynamic-update-slice_fusion.42
  60.5 0.1 bitcast_dynamic-update-slice_fusion.43
  61.1 0.2 broadcast_multiply_fusion.3
  61.2 1.6 %slice_add_fusion.81 = f32[16,128,136]{2,1,0:T(8,128)S(1)} fusion(f32[16,136,136]{2,1,0:T(8,128)S(1)} %broadcast_multiply_fusion.3), kind=kLoop, calls=%fused_computation.9.clone.1 | loop fusion | flops 2228224 | bytes 11141120 | tf_op jit(solution)/shard_map/while/body/eval_jaxpr/add | solution.py:49
  62.8 3.0 %fusion.19 = bf16[128,128,128]{2,1,0:T(8,128)(2,1)} fusion(bf16[128,128,128]{2,1,0:T(8,128)(2,1)} %get-tuple-element.499, s32[]{:T(128)S(6)} %select_n.516, f32[16,128,128]{2,1,0:T(8,128)S(1)} %get-tuple-element.442, f32[16,128,128]{2,1,0:T(8,128)S(1)} %get-tuple-element.443, f32[16,128,136]{2,1,0:T(8,128)S(1)} %slice_add_fusion.81, ...), kind=kLoop, calls=%fused_computation.30.clone.1 | loop fusion | flops 4980736 | bytes 12189700 | tf_op jit(solution)/shard_map/while/body/eval_jaxpr/dynamic_update_slice | solution.py:85
  70.7 0.2 broadcast_multiply_fusion.3
  70.8 1.6 %slice_add_fusion.81 = f32[16,128,136]{2,1,0:T(8,128)S(1)} fusion(f32[16,136,136]{2,1,0:T(8,128)S(1)} %broadcast_multiply_fusion.3), kind=kLoop, calls=%fused_computation.9.clone.1 | loop fusion | flops 2228224 | bytes 11141120 | tf_op jit(solution)/shard_map/while/body/eval_jaxpr/add | solution.py:49
  72.4 3.0 %fusion.19 = bf16[128,128,128]{2,1,0:T(8,128)(2,1)} fusion(bf16[128,128,128]{2,1,0:T(8,128)(2,1)} %get-tuple-element.499, s32[]{:T(128)S(6)} %select_n.516, f32[16,128,128]{2,1,0:T(8,128)S(1)} %get-tuple-element.442, f32[16,128,128]{2,1,0:T(8,128)S(1)} %get-tuple-element.443, f32[16,128,136]{2,1,0:T(8,128)S(1)} %slice_add_fusion.81, ...), kind=kLoop, calls=%fused_computation.30.clone.1 | loop fusion | flops 4980736 | bytes 12189700 | tf_op jit(solution)/shard_map/while/body/eval_jaxpr/dynamic_update_slice | solution.py:85
  80.3 0.2 broadcast_multiply_fusion.3
  80.4 1.6 %slice_add_fusion.81 = f32[16,128,136]{2,1,0:T(8,128)S(1)} fusion(f32[16,136,136]{2,1,0:T(8,128)S(1)} %broadcast_multiply_fusion.3), kind=kLoop, calls=%fused_computation.9.clone.1 | loop fusion | flops 2228224 | bytes 11141120 | tf_op jit(solution)/shard_map/while/body/eval_jaxpr/add | solution.py:49
  82.0 3.0 %fusion.19 = bf16[128,128,128]{2,1,0:T(8,128)(2,1)} fusion(bf16[128,128,128]{2,1,0:T(8,128)(2,1)} %get-tuple-element.499, s32[]{:T(128)S(6)} %select_n.516, f32[16,128,128]{2,1,0:T(8,128)S(1)} %get-tuple-element.442, f32[16,128,128]{2,1,0:T(8,128)S(1)} %get-tuple-element.443, f32[16,128,136]{2,1,0:T(8,128)S(1)} %slice_add_fusion.81, ...), kind=kLoop, calls=%fused_computation.30.clone.1 | loop fusion | flops 4980736 | bytes 12189700 | tf_op jit(solution)/shard_map/while/body/eval_jaxpr/dynamic_update_slice | solution.py:85
  89.9 0.2 broadcast_multiply_fusion.3
  90.0 1.6 %slice_add_fusion.81 = f32[16,128,136]{2,1,0:T(8,128)S(1)} fusion(f32[16,136,136]{2,1,0:T(8,128)S(1)} %broadcast_multiply_fusion.3), kind=kLoop, calls=%fused_computation.9.clone.1 | loop fusion | flops 2228224 | bytes 11141120 | tf_op jit(solution)/shard_map/while/body/eval_jaxpr/add | solution.py:49
  91.6 3.0 %fusion.19 = bf16[128,128,128]{2,1,0:T(8,128)(2,1)} fusion(bf16[128,128,128]{2,1,0:T(8,128)(2,1)} %get-tuple-element.499, s32[]{:T(128)S(6)} %select_n.516, f32[16,128,128]{2,1,0:T(8,128)S(1)} %get-tuple-element.442, f32[16,128,128]{2,1,0:T(8,128)S(1)} %get-tuple-element.443, f32[16,128,136]{2,1,0:T(8,128)S(1)} %slice_add_fusion.81, ...), kind=kLoop, calls=%fused_computation.30.clone.1 | loop fusion | flops 4980736 | bytes 12189700 | tf_op jit(solution)/shard_map/while/body/eval_jaxpr/dynamic_update_slice | solution.py:85
  99.5 0.2 broadcast_multiply_fusion.3
  99.6 1.6 %slice_add_fusion.81 = f32[16,128,136]{2,1,0:T(8,128)S(1)} fusion(f32[16,136,136]{2,1,0:T(8,128)S(1)} %broadcast_multiply_fusion.3), kind=kLoop, calls=%fused_computation.9.clone.1 | loop fusion | flops 2228224 | bytes 11141120 | tf_op jit(solution)/shard_map/while/body/eval_jaxpr/add | solution.py:49
  101.2 3.0 %fusion.19 = bf16[128,128,128]{2,1,0:T(8,128)(2,1)} fusion(bf16[128,128,128]{2,1,0:T(8,128)(2,1)} %get-tuple-element.499, s32[]{:T(128)S(6)} %select_n.516, f32[16,128,128]{2,1,0:T(8,128)S(1)} %get-tuple-element.442, f32[16,128,128]{2,1,0:T(8,128)S(1)} %get-tuple-element.443, f32[16,128,136]{2,1,0:T(8,128)S(1)} %slice_add_fusion.81, ...), kind=kLoop, calls=%fused_computation.30.clone.1 | loop fusion | flops 4980736 | bytes 12189700 | tf_op jit(solution)/shard_map/while/body/eval_jaxpr/dynamic_update_slice | solution.py:85
  109.1 0.2 broadcast_multiply_fusion.3
  109.2 1.6 %slice_add_fusion.81 = f32[16,128,136]{2,1,0:T(8,128)S(1)} fusion(f32[16,136,136]{2,1,0:T(8,128)S(1)} %broadcast_multiply_fusion.3), kind=kLoop, calls=%fused_computation.9.clone.1 | loop fusion | flops 2228224 | bytes 11141120 | tf_op jit(solution)/shard_map/while/body/eval_jaxpr/add | solution.py:49
  110.8 3.0 %fusion.19 = bf16[128,128,128]{2,1,0:T(8,128)(2,1)} fusion(bf16[128,128,128]{2,1,0:T(8,128)(2,1)} %get-tuple-element.499, s32[]{:T(128)S(6)} %select_n.516, f32[16,128,128]{2,1,0:T(8,128)S(1)} %get-tuple-element.442, f32[16,128,128]{2,1,0:T(8,128)S(1)} %get-tuple-element.443, f32[16,128,136]{2,1,0:T(8,128)S(1)} %slice_add_fusion.81, ...), kind=kLoop, calls=%fused_computation.30.clone.1 | loop fusion | flops 4980736 | bytes 12189700 | tf_op jit(solution)/shard_map/while/body/eval_jaxpr/dynamic_update_slice | solution.py:85
  118.7 0.2 broadcast_multiply_fusion.3
  118.8 1.6 %slice_add_fusion.81 = f32[16,128,136]{2,1,0:T(8,128)S(1)} fusion(f32[16,136,136]{2,1,0:T(8,128)S(1)} %broadcast_multiply_fusion.3), kind=kLoop, calls=%fused_computation.9.clone.1 | loop fusion | flops 2228224 | bytes 11141120 | tf_op jit(solution)/shard_map/while/body/eval_jaxpr/add | solution.py:49
  120.4 3.0 %fusion.19 = bf16[128,128,128]{2,1,0:T(8,128)(2,1)} fusion(bf16[128,128,128]{2,1,0:T(8,128)(2,1)} %get-tuple-element.499, s32[]{:T(128)S(6)} %select_n.516, f32[16,128,128]{2,1,0:T(8,128)S(1)} %get-tuple-element.442, f32[16,128,128]{2,1,0:T(8,128)S(1)} %get-tuple-element.443, f32[16,128,136]{2,1,0:T(8,128)S(1)} %slice_add_fusion.81, ...), kind=kLoop, calls=%fused_computation.30.clone.1 | loop fusion | flops 4980736 | bytes 12189700 | tf_op jit(solution)/shard_map/while/body/eval_jaxpr/dynamic_update_slice | solution.py:85
  (397 shorter events, 35.4 us)
Async XLA Ops:
  6.5 5.3 %copy-start = (bf16[1,128,640]{2,1,0:T(8,128)(2,1)S(1)}, bf16[1,128,640]{2,1,0:T(8,128)(2,1)}, u32[]{:S(2)}) copy-start(bf16[1,128,640]{2,1,0:T(8,128)(2,1)} %param.9) | copy-start | bytes 491524
  6.5 12.0 %sort.55.cloned.1.call-start = ((), (), s32[]{:S(2)}) async-start(), calls=%async_computation.1 | async-start | bytes 24608 | tf_op jit(solution)/shard_map/jit(argsort)/sort | solution.py:122
  13.3 11.1 %all-to-all-start = ((bf16[8,16,640]{2,1,0:T(8,128)(2,1)}), bf16[8,16,640]{2,1,0:T(8,128)(2,1)S(1)}, u32[]{:S(2)}, u32[]{:S(2)}) async-start(bf16[8,16,640]{2,1,0:T(8,128)(2,1)} %bitcast.55), calls=%async_computation | async-start | bytes 327680 | tf_op jit(solution)/shard_map/all_to_all | solution.py:117
  18.5 1.9 %copy-start.1 = (s32[8,128]{1,0:T(8,128)S(1)}, s32[8,128]{1,0:T(8,128)}, u32[]{:S(2)}) copy-start(s32[8,128]{1,0:T(8,128)} %get-tuple-element.350) | copy-start | bytes 12292
  20.4 10.5 %copy-start.2 = (s32[4,1]{0,1:T(1,128)S(1)}, s32[4,1]{0,1:T(1,128)}, u32[]{:S(2)}) copy-start(s32[4,1]{0,1:T(1,128)} %param.10) | copy-start | bytes 52
  25.3 3.5 %collective-permute-start.3 = (bf16[1,4,640]{2,1,0:T(4,128)(2,1)S(1)}, bf16[1,4,640]{2,1,0:T(4,128)(2,1)S(1)}, u32[]{:S(2)}, u32[]{:S(2)}) collective-permute-start(bf16[1,4,640]{2,1,0:T(4,128)(2,1)S(1)} %get-tuple-element.381), channel_id=1, source_target_pairs={{0,4},{4,8},{8,12},{12,16},{16,20},{20,24},{24,28},{1,5},{5,9},{9,... | collective-permute-start | bytes 15368 | tf_op jit(solution)/shard_map/ppermute | solution.py:35
  26.9 3.8 %collective-permute-start.4 = (bf16[1,4,640]{2,1,0:T(4,128)(2,1)S(1)}, bf16[1,4,640]{2,1,0:T(4,128)(2,1)S(1)}, u32[]{:S(2)}, u32[]{:S(2)}) collective-permute-start(bf16[1,4,640]{2,1,0:T(4,128)(2,1)S(1)} %get-tuple-element.382), channel_id=1, source_target_pairs={{4,0},{8,4},{12,8},{16,12},{20,16},{24,20},{28,24},{5,1},{9,5},{13... | collective-permute-start | bytes 15368 | tf_op jit(solution)/shard_map/ppermute | solution.py:37
  33.6 6.7 %collective-permute-start.2 = (bf16[136,264]{1,0:T(8,128)(2,1)S(1)}, bf16[136,264]{1,0:T(8,128)(2,1)}, u32[]{:S(2)}, u32[]{:S(2)}) collective-permute-start(bf16[136,264]{1,0:T(8,128)(2,1)S(1)} %constant_dynamic-slice_fusion.4), channel_id=1, source_target_pairs={{0,1},{1,2},{2,3},{3,0},{4,5},{5,6},{6,7},{7,4},{8,9},{9,10},{10,1... | collective-permute-start | bytes 215432 | tf_op jit(solution)/shard_map/cond/branch_2_fun/ppermute | solution.py:24
Sparse Core Ops, SparseCore 0:
  9.6 2.2 sort.57.cloned.1.call-done
  (1 shorter events, 0.0 us)
where the time goes:
time: 132 us; the launch traced here: 130 us
  other arithmetic  50.5 us (38%)
  local copies, waits for them, and re-layouts  43.5 us (33%)
  between operations  14.2 us (11%)
  starting transfers between devices  9.63 us (7%)
  waiting for transfers between devices  8.16 us (6%)
  loops' own time  4.32 us (3%)
    while x360, local copies, waits for them, and re-layouts  34.4 us
    dynamic_update_slice x8, other arithmetic, block_step(): lax.dynamic_update_slice_in_dim(volume, ncc_score.astype(jnp.bfloat16), f...  24.2 us
    add x11, other arithmetic, box_sum(): row_sums = row_sums + values[..., shift_row:shift_row + out_rows, :]  13.3 us
    all_to_all x1, starting transfers between devices, shards(): lax.all_to_all(outgoing, 'strip', split_axis=0, concat_axis=0, tiled=True)  5.17 us
    ppermute x1, waiting for transfers between devices, passed_along(): lax.ppermute(value, axis, [(i, (i + by) % size) for i in range(size)])  5.07 us
    broadcast_in_dim x1, local copies, waits for them, and re-layouts, cost_block(): empty = jnp.zeros((DISP, rows_out, cols_out), jnp.bfloat16)  3.06 us
  transfers between devices with their start and end apart: 4, of which 3 were waited for; matrix products, arithmetic and copies ran while one was open for 4% of the time, Pallas kernels for 0%

commit v1 on v0

--- a/solution.py
+++ b/solution.py
@@ -1,6 +1,10 @@
+import functools
+
 import jax
 import jax.numpy as jnp
 from jax import lax
+from jax.experimental import pallas as pl
+from jax.experimental.pallas import tpu as pltpu
 from jax.sharding import PartitionSpec as P
 
 COLS = 128
@@ -41,53 +45,139 @@
     return cells
 
 
-def box_sum(values):
-    out_rows = values.shape[-2] - 8
-    out_cols = values.shape[-1] - 8
-    row_sums = values[..., 0:out_rows, :]
-    for shift_row in range(1, 9):
-        row_sums = row_sums + values[..., shift_row : shift_row + out_rows, :]
-    box_total = row_sums[..., 0:out_cols]
-    for shift_col in range(1, 9):
-        box_total = box_total + row_sums[..., shift_col : shift_col + out_cols]
-    return box_total
-
-
-def cost_block(ref_window, mate_window):
-    ref_float = ref_window.astype(jnp.float32)
-    mate_float = mate_window.astype(jnp.float32)
-    rows_out = ref_window.shape[0] - 8
-    cols_out = ref_window.shape[1] - 8
-    sum_ref = box_sum(ref_float)
-    sum_ref_sq = box_sum(ref_float * ref_float)
-    mean_ref = sum_ref / 81.0
-    var_ref = sum_ref_sq / 81.0 - mean_ref * mean_ref
-    mate_box = box_sum(mate_float)
-    mate_box_sq = box_sum(mate_float * mate_float)
-
-    def block_step(block_index, volume):
-        first_disp = (block_index * 16).astype(jnp.int32)
-        starts = [DISP - 1 - within - first_disp for within in range(16)]
-        shifted = jnp.stack(
-            [lax.dynamic_slice_in_dim(mate_float, begin, cols_out + 8, 1) for begin in starts]
-        )
-        sum_cross = box_sum(ref_float[None] * shifted)
-        sum_mate = jnp.stack(
-            [lax.dynamic_slice_in_dim(mate_box, begin, cols_out, 1) for begin in starts]
-        )
-        sum_mate_sq = jnp.stack(
-            [lax.dynamic_slice_in_dim(mate_box_sq, begin, cols_out, 1) for begin in starts]
-        )
-        mean_mate = sum_mate / 81.0
-        var_mate = sum_mate_sq / 81.0 - mean_mate * mean_mate
-        covariance = sum_cross / 81.0 - mean_ref * mean_mate
-        ncc_score = covariance * lax.rsqrt((var_ref + EPSILON) * (var_mate + EPSILON))
-        return lax.dynamic_update_slice_in_dim(
-            volume, ncc_score.astype(jnp.bfloat16), first_disp, 0
-        )
-
-    empty = jnp.zeros((DISP, rows_out, cols_out), jnp.bfloat16)
-    return lax.fori_loop(0, DISP // 16, block_step, empty)
+RB=16
+UN=8
+PITCH=17
+
+def cost_kernel(ref_ref, mate_ref, out_ref, ref32, mate32, H, S, hm, hq, rm, ra, *, rows):
+    g = pl.program_id(0)
+    f32=jnp.float32; bf=jnp.bfloat16
+    i0 = lax.broadcasted_iota(jnp.int32,(128,128),0)
+    i1 = lax.broadcasted_iota(jnp.int32,(128,128),1)
+    d1 = i1 - i0
+    band1 = ((d1>=0)&(d1<=8)).astype(bf)
+    d2 = 16 + i1 - i0
+    band2 = ((d2>=0)&(d2<=8)&(i1>=112)).astype(bf)
+
+    @pl.when(g==0)
+    def _():
+        ref32[...] = ref_ref[...].astype(f32)
+        mate32[...] = mate_ref[...].astype(f32)
+        kk = lax.broadcasted_iota(jnp.int32,(384,256),0)
+        cc = lax.broadcasted_iota(jnp.int32,(384,256),1)
+        box = ((kk-cc>=0)&(kk-cc<=8)).astype(bf)
+        def boxes(x, w):
+            p = x.astype(f32)*x.astype(f32)
+            hi = p.astype(bf)
+            lo = (p - hi.astype(f32)).astype(bf)
+            s = jnp.dot(x, w, preferred_element_type=f32)
+            q = jnp.dot(hi, w, preferred_element_type=f32)+jnp.dot(lo, w, preferred_element_type=f32)
+            return s,q
+        s,q = boxes(mate_ref[...], box)
+        hm[0] = s[:, :128]; hm[1]=s[:,128:]; hq[0] = q[:, :128]; hq[1]=q[:,128:]
+        kr = lax.broadcasted_iota(jnp.int32,(256,128),0)
+        cr = lax.broadcasted_iota(jnp.int32,(256,128),1)
+        dr = jnp.where(kr<128, kr, kr-112) - cr
+        boxr = ((dr>=0)&(dr<=8)&((kr<128)|(kr>=240))).astype(bf)
+        s,q = boxes(ref_ref[...], boxr)
+        rm[...] = s; ra[...] = q
+
+    def one_row(r):
+        m = jnp.broadcast_to(mate32[pl.ds(r,1),:], (16,384))
+        base = pltpu.roll(m, 1, axis=1, stride=1, stride_axis=0).astype(bf)
+        t = [base[:, 128*i:128*i+128] for i in range(3)]
+        lane = lax.broadcasted_iota(jnp.int32,(16,128),1)
+        tiles=[]
+        for p in range(-1,8):
+            o = 128-16*p
+            a, b = divmod(o,128)
+            if b==0:
+                w = t[a]
+            else:
+                w = jnp.where(lane>=b, t[a], t[a+1])
+                w = pltpu.roll(w.astype(f32), 128-b, axis=1).astype(bf)
+            tiles.append(w)
+        left = jnp.concatenate(tiles[1:],axis=0)
+        right = jnp.concatenate(tiles[:-1],axis=0)
+        rr = ref32[pl.ds(r,1),:].astype(bf)
+        w1 = band1*jnp.broadcast_to(rr[:, :128],(128,128))
+        rsh = rr[:, 128:]
+        w2 = band2*jnp.broadcast_to(rsh,(128,128))
+        lhs = jnp.concatenate([left,right],axis=1)
+        rhs = jnp.concatenate([w1,w2],axis=1)
+        return lax.dot_general(lhs, rhs, (((1,),(1,)),((),())), preferred_element_type=f32)
+
+    lo = jnp.where(g==0, 0, (RB*g+8)//UN)
+    hi = (RB*g+RB+8)//UN
+    def body(it, c):
+        for j in range(UN):
+            r = it*UN+j
+            H[r] = one_row(r)
+        return c
+    lax.fori_loop(lo, hi, body, 0)
+
+    r0 = RB*g
+    def vq(q, c):
+        h = [H[r0+i, pl.ds(pl.multiple_of(8*q,8),8), :] for i in range(RB+8)]
+        out=[None]*RB
+        for b0 in range(0, RB, 9):
+            n = min(9, RB-b0)
+            suf=[None]*9
+            suf[8]=h[b0+8]
+            for i in range(7,-1,-1): suf[i]=h[b0+i]+suf[i+1]
+            out[b0]=suf[0]
+            pre=None
+            for i in range(1,n):
+                pre = h[b0+8+i] if pre is None else pre+h[b0+8+i]
+                out[b0+i]=suf[i]+pre
+        for i in range(RB):
+            S[pl.ds(8*q*PITCH+i, 8, stride=PITCH), :] = out[i]
+        return c
+    lax.fori_loop(0, 16, vq, 0)
+
+    def vert(ref):
+        x = [ref[pl.ds(r0+i, RB), :] for i in range(9)]
+        return ((x[0]+x[1])+(x[2]+x[3]))+((x[4]+x[5])+(x[6]+x[7]))+x[8]
+    sr = vert(rm); srr = vert(ra)
+    mr = sr/81.0
+    ar = lax.rsqrt(jnp.maximum(srr/81.0-mr*mr,0.0)+EPSILON)
+    sm0 = vert(hm.at[0]); sm1=vert(hm.at[1])
+    def inv(s, q):
+        mm = s/81.0
+        return lax.rsqrt(jnp.maximum(q/81.0-mm*mm,0.0)+EPSILON)/81.0
+    am0 = inv(sm0, vert(hq.at[0])); am1 = inv(sm1, vert(hq.at[1]))
+    lane = lax.broadcasted_iota(jnp.int32,(RB,128),1)
+    for k in range(128):
+        o = 127-k
+        x, y = sm0, am0
+        if o:
+            keep = lane>=o
+            x = pltpu.roll(jnp.where(keep, sm0, sm1), 128-o, axis=1)
+            y = pltpu.roll(jnp.where(keep, am0, am1), 128-o, axis=1)
+        s = S[pl.ds(k*PITCH, RB), :]
+        v = (s - mr*x)*ar*y
+        out_ref[k] = v.astype(bf)
+
+def cost(ref_in, mate_in):
+    rows = ref_in.shape[0]-8
+    f32=jnp.float32
+    return pl.pallas_call(
+        functools.partial(cost_kernel, rows=rows),
+        out_shape=jax.ShapeDtypeStruct((DISP, rows, COLS), jnp.bfloat16),
+        grid=(rows//RB,),
+        in_specs=[pl.BlockSpec((rows+8,256), lambda g:(0,0)), pl.BlockSpec((rows+8,384), lambda g:(0,0))],
+        out_specs=pl.BlockSpec((DISP, RB, COLS), lambda g:(0,g,0)),
+        scratch_shapes=[pltpu.VMEM((rows+8,256),f32), pltpu.VMEM((rows+8,384),f32),
+            pltpu.VMEM((rows+8,128,128),f32), pltpu.VMEM((128*PITCH,128),f32),
+            pltpu.VMEM((2,rows+8,128),f32), pltpu.VMEM((2,rows+8,128),f32),
+            pltpu.VMEM((rows+8,128),f32), pltpu.VMEM((rows+8,128),f32)],
+        compiler_params=pltpu.CompilerParams(dimension_semantics=("arbitrary",), vmem_limit_bytes=48<<20),
+        name="cost_volume",
+    )(ref_in, mate_in)
+
+def prep(ref_window, mate_window):
+    r = jnp.concatenate([ref_window[:, :128], jnp.pad(ref_window[:, 16:136],((0,0),(0,8)))], axis=1)
+    return r, jnp.pad(mate_window, ((0,0),(0,120)))
 
 
 def rotate_by(step_size, view_me, view_count, offsets, span_cols):
@@ -132,7 +222,7 @@
     ]
     mate_window = lax.switch(step_now - 1, branches, own_rows)
     ref_window = own_rows[:, OFF_MAX + DISP - 1 : OFF_MAX + DISP - 1 + COLS + 8]
-    volume = cost_block(ref_window, mate_window)
+    volume = cost(*prep(ref_window, mate_window))
     return volume[None]
 
 

time: 132 us -> 65.6 us (0.50)
  the two profiles are of different devices: /device:TPU:0 before, /device:TPU:5 now
where the time goes in v1:
time: 65.6 us; the launch traced here: 65.8 us
  Pallas kernels  16.6 us (25%)
  between operations  14.2 us (22%)
  starting transfers between devices  12.2 us (19%)
  other arithmetic  8.66 us (13%)
  waiting for transfers between devices  7.77 us (12%)
  local copies, waits for them, and re-layouts  4.56 us (7%)
  loops' own time  1.86 us (3%)
    pallas_call x1, Pallas kernels, cost(): pl.pallas_call(functools.partial(cost_kernel, rows=rows), out_shape=jax.S...  16.6 us
    ppermute x1, waiting for transfers between devices, passed_along(): lax.ppermute(value, axis, [(i, (i + by) % size) for i in range(size)])  5.44 us
    all_to_all x1, starting transfers between devices, shards(): lax.all_to_all(outgoing, 'strip', split_axis=0, concat_axis=0, tiled=True)  4.54 us
    ppermute x1, starting transfers between devices, with_halo(): lax.ppermute(tail, axis, [(i, (i + 1) % count) for i in range(ends)])  3.34 us
    sort x1, other arithmetic, shards(): inverse = jnp.argsort(slot_ids)  2.57 us
    sort x1, other arithmetic, shards(): send_order = jnp.argsort(targets, stable=True)  2.54 us
    ppermute x1, starting transfers between devices, passed_along(): lax.ppermute(value, axis, [(i, (i + by) % size) for i in range(size)])  2.37 us
    ppermute x1, waiting for transfers between devices, with_halo(): lax.ppermute(head, axis, [((i + 1) % count, i) for i in range(ends)])  2.33 us
  transfers between devices with their start and end apart: 4, of which 2 were waited for; matrix products, arithmetic and copies ran while one was open for 7% of the time, Pallas kernels for 0%

profile of v1, /device:TPU:5, one launch (start us, length us, event | category | flops | bytes accessed | tf_op | source)
XLA Modules:
  0.0 65.8 jit_solution(7142326686873965183)
XLA Ops:
  6.5 0.0 copy-start
  6.5 0.0 copy-start.2
  6.5 0.0 sort.55.cloned.1.call-start
  6.6 1.3 %iota_select_fusion = (s32[8,128]{1,0:T(8,128)}, s32[8,128]{1,0:T(8,128)S(1)}) fusion(s32[1024]{0:T(1024)} %param.10, s32[128]{0:T(128)S(1)} %iota_add_fusion, s32[]{:T(128)S(6)} %axis_index.23), kind=kLoop, calls=%fused_computation.26 | loop fusion | flops 21504 | bytes 12804 | tf_op jit(solution)/shard_map/jit(_where)/select_n | solution.py:211
  7.9 0.6 iota.27
  8.5 0.0 sort.55.cloned.1.call-update
  8.5 0.8 %and_select_fusion.1 = s32[128]{0:T(128)S(1)} fusion(s32[1024]{0:T(1024)} %param.10, s32[]{:T(128)S(6)} %select_n.77), kind=kLoop, calls=%fused_computation.32 | loop fusion | flops 1920 | bytes 1028 | tf_op jit(solution)/shard_map/jit(floor_divide)/jit(_where)/select_n | solution.py:204
  9.3 2.5 %sort.51 = (s32[128]{0:T(128)}, s32[128]{0:T(128)S(1)}) sort(s32[128]{0:T(128)S(1)} %and_select_fusion.1, s32[128]{0:T(128)S(1)} %iota.23), dimensions={0}, to_apply=%region_0.1 | sort | flops 896 | bytes 2048 | tf_op jit(solution)/shard_map/jit(argsort)/sort | solution.py:205
  11.8 0.0 copy-done
  11.8 1.5 %gather_fusion = bf16[128,640]{1,0:T(8,128)(2,1)} fusion(bf16[128,640]{1,0:T(8,128)(2,1)S(1)} %bitcast.49, s32[1024]{0:T(1024)S(1)} %pad_clamp_fusion.1), kind=kCustom, calls=%fused_computation | custom fusion | bytes 328192 | tf_op jit(solution)/shard_map/gather | solution.py:206
  13.4 4.5 %all-to-all-start = ((bf16[8,16,640]{2,1,0:T(8,128)(2,1)}), bf16[8,16,640]{2,1,0:T(8,128)(2,1)S(1)}, u32[]{:S(2)}, u32[]{:S(2)}) async-start(bf16[8,16,640]{2,1,0:T(8,128)(2,1)} %bitcast.7), calls=%async_computation | async-start | bytes 327680 | tf_op jit(solution)/shard_map/all_to_all | solution.py:207
  17.9 0.0 sort.55.cloned.1.call-done
  17.9 0.0 copy-start.1
  17.9 0.8 %bitcast_or_fusion = s32[8,16,1]{1,0,2:T(8,128)S(1)} fusion(s32[8,128]{1,0:T(8,128)} %get-tuple-element.41), kind=kLoop, calls=%fused_computation.22 | loop fusion | flops 1024 | bytes 1024 | tf_op jit(solution)/shard_map/jit(take_along_axis)/gather | solution.py:213
  18.7 0.1 reshape.55
  18.8 1.0 %gather_fusion.2 = s32[128]{0:T(128)S(1)} fusion(s32[8,128]{1,0:T(8,128)S(1)} %get-tuple-element.52, s32[128]{0:T(128)S(1)} %reshape.55), kind=kCustom, calls=%fused_computation.2 | custom fusion | bytes 2048 | tf_op jit(solution)/shard_map/jit(take_along_axis)/gather | solution.py:213
  19.8 0.1 reshape.58
  19.8 0.0 copy-done.1
  19.8 0.1 select_n.85
  19.9 2.6 %sort.53 = (s32[128]{0:T(128)}, s32[128]{0:T(128)S(1)}) sort(s32[128]{0:T(128)S(1)} %select_n.85, s32[128]{0:T(128)S(1)} %iota.28), dimensions={0}, to_apply=%region_2.3 | sort | flops 896 | bytes 2048 | tf_op jit(solution)/shard_map/jit(argsort)/sort | solution.py:214
  22.5 0.0 all-to-all-done
  22.5 0.9 %gather_fusion.1 = bf16[128,640]{1,0:T(8,128)(2,1)S(1)} fusion(bf16[128,640]{1,0:T(8,128)(2,1)S(1)} %bitcast.50, s32[1024]{0:T(1024)S(1)} %pad_clamp_fusion), kind=kCustom, calls=%fused_computation.1 | custom fusion | bytes 328192 | tf_op jit(solution)/shard_map/gather | solution.py:215
  23.4 3.3 %collective-permute-start.3 = (bf16[1,4,640]{2,1,0:T(4,128)(2,1)S(1)}, bf16[1,4,640]{2,1,0:T(4,128)(2,1)S(1)}, u32[]{:S(2)}, u32[]{:S(2)}) collective-permute-start(bf16[1,4,640]{2,1,0:T(4,128)(2,1)S(1)} %get-tuple-element.49), channel_id=1, source_target_pairs={{0,4},{4,8},{8,12},{12,16},{16,20},{20,24},{24,28},{1,5},{5,9},{9,... | collective-permute-start | bytes 15368 | tf_op jit(solution)/shard_map/ppermute | solution.py:39
  26.8 1.9 %collective-permute-start.4 = (bf16[1,4,640]{2,1,0:T(4,128)(2,1)S(1)}, bf16[1,4,640]{2,1,0:T(4,128)(2,1)S(1)}, u32[]{:S(2)}, u32[]{:S(2)}) collective-permute-start(bf16[1,4,640]{2,1,0:T(4,128)(2,1)S(1)} %get-tuple-element.50), channel_id=1, source_target_pairs={{4,0},{8,4},{12,8},{16,12},{20,16},{24,20},{28,24},{5,1},{9,5},{13... | collective-permute-start | bytes 15368 | tf_op jit(solution)/shard_map/ppermute | solution.py:41
  29.4 0.0 collective-permute-done.3
  29.4 2.3 %collective-permute-done.4 = bf16[1,4,640]{2,1,0:T(4,128)(2,1)S(1)} collective-permute-done((bf16[1,4,640]{2,1,0:T(4,128)(2,1)S(1)}, bf16[1,4,640]{2,1,0:T(4,128)(2,1)S(1)}, u32[]{:S(2)}, u32[]{:S(2)}) %collective-permute-start.4) | collective-permute-done | bytes 5152 | tf_op jit(solution)/shard_map/ppermute | solution.py:41
  31.7 0.1 maximum_bitcast_fusion
  31.8 0.1 slice.32
  31.8 0.1 slice.31
  31.9 0.0 copy-done.2
  32.0 10.4 %conditional.1 = (bf16[136,384]{1,0:T(8,128)(2,1)S(1)}) conditional(s32[]{:T(128)} %clamp.3, (s32[]{:T(128)}, s32[4,1]{0,1:T(1,128)S(1)}, bf16[136,640]{1,0:T(8,128)(2,1)S(1)}) %tuple.29, (s32[]{:T(128)}, s32[4,1]{0,1:T(1,128)S(1)}, bf16[136,640]{1,0:T(8,128)(2,1)S(1)}) %tuple.30, (s32[]{:T(128)}, s32[4,1]{0,1:T(1,128)S(1)}, ...), branch_computations={%region_3.4_spmd, %region_4.5_spmd, %region_5.6_spmd} | conditional | flops 19 | bytes 607363 | solution.py:223
  32.0 0.6 fusion.7
  34.4 0.1 constant_dynamic-slice_fusion.2
  34.5 2.4 %collective-permute-start.1 = (bf16[136,264]{1,0:T(8,128)(2,1)S(1)}, bf16[136,264]{1,0:T(8,128)(2,1)S(1)}, u32[]{:S(2)}, u32[]{:S(2)}) collective-permute-start(bf16[136,264]{1,0:T(8,128)(2,1)S(1)} %constant_dynamic-slice_fusion.2), channel_id=1, source_target_pairs={{0,2},{1,3},{2,0},{3,1},{4,6},{5,7},{6,4},{7,5},{8,10},{9,11},{10,... | collective-permute-start | bytes 215432 | tf_op jit(solution)/shard_map/cond/branch_1_fun/ppermute | solution.py:28
  36.9 5.4 %collective-permute-done.1 = bf16[136,264]{1,0:T(8,128)(2,1)S(1)} collective-permute-done((bf16[136,264]{1,0:T(8,128)(2,1)S(1)}, bf16[136,264]{1,0:T(8,128)(2,1)S(1)}, u32[]{:S(2)}, u32[]{:S(2)}) %collective-permute-start.1) | collective-permute-done | bytes 71840 | tf_op jit(solution)/shard_map/cond/branch_1_fun/ppermute | solution.py:28
  42.4 16.6 %cost_volume.1 = bf16[128,128,128]{2,1,0:T(8,128)(2,1)} custom-call(bf16[136,256]{1,0:T(8,128)(2,1)S(1)} %fusion.1.ref_ref, bf16[136,384]{1,0:T(8,128)(2,1)S(1)} %get-tuple-element.55.mate_ref), custom_call_target="tpu_custom_call" | custom-call | tf_op jit(solution)/shard_map/cost_volume/pallas_call | solution.py:164
  (11 shorter events, 0.1 us)
Async XLA Ops:
  6.5 5.3 %copy-start = (bf16[1,128,640]{2,1,0:T(8,128)(2,1)S(1)}, bf16[1,128,640]{2,1,0:T(8,128)(2,1)}, u32[]{:S(2)}) copy-start(bf16[1,128,640]{2,1,0:T(8,128)(2,1)} %param.7) | copy-start | bytes 491524
  6.5 25.4 %copy-start.2 = (s32[4,1]{0,1:T(1,128)S(1)}, s32[4,1]{0,1:T(1,128)}, u32[]{:S(2)}) copy-start(s32[4,1]{0,1:T(1,128)} %param.8) | copy-start | bytes 52
  6.5 11.4 %sort.55.cloned.1.call-start = ((), (), s32[]{:S(2)}) async-start(), calls=%async_computation.1 | async-start | bytes 24608 | tf_op jit(solution)/shard_map/jit(argsort)/sort | solution.py:212
  13.4 9.1 %all-to-all-start = ((bf16[8,16,640]{2,1,0:T(8,128)(2,1)}), bf16[8,16,640]{2,1,0:T(8,128)(2,1)S(1)}, u32[]{:S(2)}, u32[]{:S(2)}) async-start(bf16[8,16,640]{2,1,0:T(8,128)(2,1)} %bitcast.7), calls=%async_computation | async-start | bytes 327680 | tf_op jit(solution)/shard_map/all_to_all | solution.py:207
  17.9 1.9 %copy-start.1 = (s32[8,128]{1,0:T(8,128)S(1)}, s32[8,128]{1,0:T(8,128)}, u32[]{:S(2)}) copy-start(s32[8,128]{1,0:T(8,128)} %get-tuple-element.41) | copy-start | bytes 12292
  23.4 5.9 %collective-permute-start.3 = (bf16[1,4,640]{2,1,0:T(4,128)(2,1)S(1)}, bf16[1,4,640]{2,1,0:T(4,128)(2,1)S(1)}, u32[]{:S(2)}, u32[]{:S(2)}) collective-permute-start(bf16[1,4,640]{2,1,0:T(4,128)(2,1)S(1)} %get-tuple-element.49), channel_id=1, source_target_pairs={{0,4},{4,8},{8,12},{12,16},{16,20},{20,24},{24,28},{1,5},{5,9},{9,... | collective-permute-start | bytes 15368 | tf_op jit(solution)/shard_map/ppermute | solution.py:39
  26.8 4.9 %collective-permute-start.4 = (bf16[1,4,640]{2,1,0:T(4,128)(2,1)S(1)}, bf16[1,4,640]{2,1,0:T(4,128)(2,1)S(1)}, u32[]{:S(2)}, u32[]{:S(2)}) collective-permute-start(bf16[1,4,640]{2,1,0:T(4,128)(2,1)S(1)} %get-tuple-element.50), channel_id=1, source_target_pairs={{4,0},{8,4},{12,8},{16,12},{20,16},{24,20},{28,24},{5,1},{9,5},{13... | collective-permute-start | bytes 15368 | tf_op jit(solution)/shard_map/ppermute | solution.py:41
  34.5 7.8 %collective-permute-start.1 = (bf16[136,264]{1,0:T(8,128)(2,1)S(1)}, bf16[136,264]{1,0:T(8,128)(2,1)S(1)}, u32[]{:S(2)}, u32[]{:S(2)}) collective-permute-start(bf16[136,264]{1,0:T(8,128)(2,1)S(1)} %constant_dynamic-slice_fusion.2), channel_id=1, source_target_pairs={{0,2},{1,3},{2,0},{3,1},{4,6},{5,7},{6,4},{7,5},{8,10},{9,11},{10,... | collective-permute-start | bytes 215432 | tf_op jit(solution)/shard_map/cond/branch_1_fun/ppermute | solution.py:28
Sparse Core Ops, SparseCore 0:
  9.6 2.2 sort.57.cloned.1.call-done
  (1 shorter events, 0.0 us)

commit v2 on v1

--- a/solution.py
+++ b/solution.py
@@ -13,36 +13,6 @@
 
 
 EPSILON = 1e-05
-
-
-def for_sending(value):
-
-    def short(part):
-        return part.astype(jnp.bfloat16) if part.dtype == jnp.float32 else part
-
-    return jax.tree.map(short, value)
-
-
-def passed_along(value, axis, by):
-    size = lax.axis_size(axis)
-    return lax.ppermute(value, axis, [(i, (i + by) % size) for i in range(size)])
-
-
-def with_halo(cells, sides, width):
-    for axis, dim in sides:
-        count = lax.axis_size(axis)
-        ends = count - 1
-        head = lax.slice_in_dim(cells, 0, width, axis=dim)
-        tail = lax.slice_in_dim(cells, cells.shape[dim] - width, cells.shape[dim], axis=dim)
-        cells = jnp.concatenate(
-            [
-                lax.ppermute(tail, axis, [(i, (i + 1) % count) for i in range(ends)]),
-                cells,
-                lax.ppermute(head, axis, [((i + 1) % count, i) for i in range(ends)]),
-            ],
-            axis=dim,
-        )
-    return cells
 
 
 RB=16
@@ -175,55 +145,116 @@
         name="cost_volume",
     )(ref_in, mate_in)
 
-def prep(ref_window, mate_window):
-    r = jnp.concatenate([ref_window[:, :128], jnp.pad(ref_window[:, 16:136],((0,0),(0,8)))], axis=1)
-    return r, jnp.pad(mate_window, ((0,0),(0,120)))
-
-
-def rotate_by(step_size, view_me, view_count, offsets, span_cols):
-
-    def branch(own_rows):
-        receiver = (view_me - step_size) % view_count
-        slab = lax.dynamic_slice_in_dim(own_rows, OFF_MAX - offsets[receiver, 0], span_cols, 1)
-        return passed_along(for_sending(slab), "view", view_count - step_size).astype(slab.dtype)
-
-    return branch
+SPAN = COLS + DISP + 8
+EDGE = 4
+REF_FROM = OFF_MAX + DISP - 1
+
+
+def slot_count(rows_dev, strips):
+    wide = rows_dev // strips + 2 * EDGE
+    return -(-wide // 8) * 8
+
+
+def places(ids, low, rows_dev):
+    line = ids.shape[1]
+    place = ids - low + EDGE
+    wanted = (place >= 0) & (place < rows_dev + 2 * EDGE)
+    before = lax.broadcasted_iota(jnp.int32, (line, line), 0)
+    after = lax.broadcasted_iota(jnp.int32, (line, line), 1)
+    earlier = (before < after).astype(jnp.bfloat16)
+    flags = jnp.where(wanted, 1.0, 0.0)
+    pad = (-flags.shape[0]) % 16
+    if pad:
+        flags = jnp.concatenate([flags, jnp.zeros((pad, line), jnp.float32)], axis=0)
+    rank = jnp.dot(flags.astype(jnp.bfloat16), earlier, preferred_element_type=jnp.float32)
+    rank = rank[: ids.shape[0]].astype(jnp.int32)
+    return jnp.where(wanted, rank, -1), place
+
+
+def spread(rank, slots):
+    strips, line = rank.shape
+    wide = jnp.broadcast_to(rank[:, None, :], (strips, slots, line))
+    return wide == lax.broadcasted_iota(jnp.int32, (strips, slots, line), 1)
+
+
+def pack_kernel(map_ref, tiles_ref, out_ref):
+    strips, slots, width = out_ref.shape
+    rows_dev = tiles_ref.shape[0]
+    ids = jnp.broadcast_to(map_ref[...], (strips, rows_dev))
+    low = rows_dev * lax.broadcasted_iota(jnp.int32, (strips, rows_dev), 0)
+    rank, _ = places(ids, low, rows_dev)
+    pick = jnp.where(spread(rank, slots), 1.0, 0.0).reshape(strips * slots, rows_dev).astype(jnp.bfloat16)
+    rows = jnp.dot(pick, tiles_ref[...], preferred_element_type=jnp.float32)
+    out_ref[...] = rows.astype(jnp.bfloat16).reshape(out_ref.shape)
+
+
+def table_kernel(table_ref, out_ref):
+    strips, rows_dev = table_ref.shape
+    rows, positions = out_ref.shape
+    slots = positions // strips
+    low = rows_dev * lax.axis_index("strip")
+    rank, place = places(table_ref[...], low, rows_dev)
+    wide = jnp.broadcast_to(place[:, None, :], (strips, slots, rows_dev))
+    named = jnp.where(spread(rank, slots), wide + 1, 0).astype(jnp.float32)
+    named = named.reshape(positions, rows_dev).astype(jnp.bfloat16)
+    ones = jnp.ones((16, rows_dev), jnp.bfloat16)
+    target = lax.dot_general(ones, named, (((1,), (1,)), ((), ())), preferred_element_type=jnp.float32)
+    target = jnp.broadcast_to(target[:1].astype(jnp.int32), (rows, positions))
+    mine = lax.broadcasted_iota(jnp.int32, (rows, positions), 0) + 1
+    out_ref[...] = jnp.where(target == mine, 1.0, 0.0).astype(jnp.bfloat16)
+
+
+def unpack_kernel(offsets_ref, step_ref, table_ref, arrived_ref, ref_ref, slab_ref, strip):
+    rows = ref_ref.shape[0]
+    width = arrived_ref.shape[1]
+    views = offsets_ref.shape[0]
+    own = jnp.dot(table_ref[...], arrived_ref[...], preferred_element_type=jnp.float32)
+    strip[:, :width] = own
+    strip[:, width:] = jnp.zeros((rows, strip.shape[1] - width), jnp.float32)
+    ref_ref[:, :128] = own[:, REF_FROM : REF_FROM + 128].astype(jnp.bfloat16)
+    ref_ref[:, 128:] = strip[:, REF_FROM + 16 : REF_FROM + 144].astype(jnp.bfloat16)
+    receiver = lax.rem(lax.axis_index("view") + views - lax.rem(step_ref[0], views), views)
+    start = jnp.clip(OFF_MAX - offsets_ref[receiver, 0], 0, OFF_MAX)
+    whole = start // 128
+    part = start - whole * 128
+    block = strip[:, pl.ds(pl.multiple_of(whole * 128, 128), 512)]
+    turned = pltpu.roll(block, 512 - part, axis=1)
+    slab_ref[...] = turned[:, :384].astype(jnp.bfloat16)
 
 
 def shards(images, offsets, pair_step, row_map):
     own_tiles = images[0]
-    rows_dev = own_tiles.shape[0]
-    width_all = own_tiles.shape[1]
-    span_cols = COLS + DISP + 8
-    strip_count = lax.axis_size("strip")
-    view_count = lax.axis_size("view")
+    rows_dev, width = own_tiles.shape
+    strips = lax.axis_size("strip")
+    views = lax.axis_size("view")
     strip_me = lax.axis_index("strip")
-    view_me = lax.axis_index("view")
-    per_peer = rows_dev // strip_count
-    local_map = lax.dynamic_slice_in_dim(row_map, strip_me * rows_dev, rows_dev)
-    targets = local_map // rows_dev
-    send_order = jnp.argsort(targets, stable=True)
-    outgoing = own_tiles[send_order].reshape(strip_count, per_peer, width_all)
+    slots = slot_count(rows_dev, strips)
+    rows = rows_dev + 2 * EDGE
+    bf16 = jnp.bfloat16
+    table = row_map.reshape(strips, rows_dev)
+    local = lax.dynamic_slice_in_dim(table, strip_me, 1)
+    outgoing = pl.pallas_call(
+        pack_kernel, out_shape=jax.ShapeDtypeStruct((strips, slots, width), bf16), name="pack"
+    )(local, own_tiles)
     arrived = lax.all_to_all(outgoing, "strip", split_axis=0, concat_axis=0, tiled=True)
-    whole_table = row_map.reshape(strip_count, rows_dev)
-    hits = whole_table // rows_dev == strip_me
-    column_ids = lax.broadcasted_iota(jnp.int32, whole_table.shape, 1)
-    rank_keys = jnp.where(hits, column_ids, column_ids + rows_dev)
-    picked = jnp.argsort(rank_keys, axis=1, stable=True)[:, :per_peer]
-    slot_ids = jnp.take_along_axis(whole_table % rows_dev, picked, axis=1).reshape(rows_dev)
-    inverse = jnp.argsort(slot_ids)
-    strip_rows = arrived.reshape(rows_dev, width_all)[inverse]
-    bordered = with_halo(strip_rows[None], (("strip", 1),), 4)
-    own_rows = bordered[0]
-    step_now = pair_step[0] % view_count
-    branches = [
-        rotate_by(step_size, view_me, view_count, offsets, span_cols)
-        for step_size in range(1, view_count)
-    ]
-    mate_window = lax.switch(step_now - 1, branches, own_rows)
-    ref_window = own_rows[:, OFF_MAX + DISP - 1 : OFF_MAX + DISP - 1 + COLS + 8]
-    volume = cost(*prep(ref_window, mate_window))
-    return volume[None]
+    select = pl.pallas_call(
+        table_kernel, out_shape=jax.ShapeDtypeStruct((rows, strips * slots), bf16), name="table"
+    )(table)
+    smem = pl.BlockSpec(memory_space=pltpu.SMEM)
+    vmem = pl.BlockSpec(memory_space=pltpu.VMEM)
+    ref_rows, slab = pl.pallas_call(
+        unpack_kernel,
+        out_shape=(jax.ShapeDtypeStruct((rows, 256), bf16), jax.ShapeDtypeStruct((rows, 384), bf16)),
+        in_specs=[smem, smem, vmem, vmem],
+        scratch_shapes=[pltpu.VMEM((rows, 768), jnp.float32)],
+        name="unpack",
+    )(offsets, pair_step, select, arrived.reshape(strips * slots, width))
+
+    def sent_by(step):
+        return lambda rows_out: lax.ppermute(rows_out, "view", [(i, (i - step) % views) for i in range(views)])
+
+    mate_rows = lax.switch(pair_step[0] % views - 1, [sent_by(step) for step in range(1, views)], slab)
+    return cost(ref_rows, mate_rows)[None]
 
 
 def solution(mesh):

time: 65.6 us -> 43.2 us (0.66)
  the two profiles are of different devices: /device:TPU:5 before, /device:TPU:0 now
where the time goes in v2:
time: 43.2 us; the launch traced here: 42.8 us
  Pallas kernels  23 us (53%)
  waiting for transfers between devices  8.17 us (19%)
  starting transfers between devices  6.75 us (16%)
  local copies, waits for them, and re-layouts  4.14 us (10%)
  between operations  0.67 us (2%)
    pallas_call x1, Pallas kernels, cost(): pl.pallas_call(functools.partial(cost_kernel, rows=rows), out_shape=jax.S...  17.5 us
    all_to_all x1, starting transfers between devices, shards(): lax.all_to_all(outgoing, 'strip', split_axis=0, concat_axis=0, tiled=True)  5.17 us
    ppermute x1, waiting for transfers between devices, sent_by(): lax.ppermute(rows_out, 'view', [(i, (i - step) % views) for i in range(vi...  5.01 us
    all_to_all x1, waiting for transfers between devices, shards(): lax.all_to_all(outgoing, 'strip', split_axis=0, concat_axis=0, tiled=True)  3.16 us
    unnamed x5, local copies, waits for them, and re-layouts  2.87 us
    pallas_call x1, Pallas kernels, shards(): pl.pallas_call(unpack_kernel, out_shape=(jax.ShapeDtypeStruct((rows, 256)...  1.95 us
    pallas_call x1, Pallas kernels, shards(): pl.pallas_call(pack_kernel, out_shape=jax.ShapeDtypeStruct((strips, slots...  1.95 us
    pallas_call x1, Pallas kernels, shards(): pl.pallas_call(table_kernel, out_shape=jax.ShapeDtypeStruct((rows, strips...  1.64 us
  transfers between devices with their start and end apart: 2, of which 2 were waited for; matrix products, arithmetic and copies ran while one was open for 3% of the time, Pallas kernels for 4%

profile of v2, /device:TPU:0, one launch (start us, length us, event | category | flops | bytes accessed | tf_op | source)
XLA Modules:
  0.0 42.8 jit_solution(10145686672271478728)
XLA Ops:
  0.0 1.3 %constant_dynamic-slice_fusion.map_ref = s32[1,128]{1,0:T(1,128)} fusion(s32[8,128]{1,0:T(8,128)} %bitcast.10, s32[]{:T(128)S(6)} %select_n.10), kind=kLoop, calls=%fused_computation | loop fusion | bytes 1028 | tf_op jit(solution)/shard_map/dynamic_slice | solution.py:235
  1.3 1.9 %pack.1 = bf16[8,24,640]{2,1,0:T(8,128)(2,1)} custom-call(s32[1,128]{1,0:T(1,128)} %constant_dynamic-slice_fusion.map_ref, bf16[128,640]{1,0:T(8,128)(2,1)} %bitcast.9), custom_call_target="tpu_custom_call" | custom-call | tf_op jit(solution)/shard_map/pack/pallas_call | solution.py:236
  3.2 5.2 %all-to-all-start = ((bf16[8,24,640]{2,1,0:T(8,128)(2,1)}), bf16[8,24,640]{2,1,0:T(8,128)(2,1)S(1)}, u32[]{:S(2)}, u32[]{:S(2)}) async-start(bf16[8,24,640]{2,1,0:T(8,128)(2,1)} %pack.1), calls=%async_computation | async-start | bytes 491520 | tf_op jit(solution)/shard_map/all_to_all | solution.py:239
  9.1 1.6 %table.1.table_ref = bf16[136,192]{1,0:T(8,128)(2,1)} custom-call(s32[8,128]{1,0:T(8,128)} %bitcast.11), custom_call_target="tpu_custom_call" | custom-call | tf_op jit(solution)/shard_map/table/pallas_call | solution.py:240
  10.7 1.3 %copy.5.offsets_ref = s32[4,1]{1,0:T(4,128)} copy(s32[4,1]{0,1:T(1,128)} %param.8) | data formatting | bytes 32 | tf_op args[1]
  12.0 3.2 %all-to-all-done = bf16[8,24,640]{2,1,0:T(8,128)(2,1)S(1)} async-done(((bf16[8,24,640]{2,1,0:T(8,128)(2,1)}), bf16[8,24,640]{2,1,0:T(8,128)(2,1)S(1)}, u32[]{:S(2)}, u32[]{:S(2)}) %all-to-all-start) | async-done | bytes 245792 | tf_op jit(solution)/shard_map/all_to_all | solution.py:239
  15.2 0.0 copy-start.1
  15.2 0.7 %copy-done.1 = bf16[8,24,640]{2,1,0:T(8,128)(2,1)} copy-done((bf16[8,24,640]{2,1,0:T(8,128)(2,1)}, bf16[8,24,640]{2,1,0:T(8,128)(2,1)S(1)}, u32[]{:S(2)}) %copy-start.1) | copy-done | bytes 245784
  15.8 2.0 %unpack.1 = (bf16[136,256]{1,0:T(8,128)(2,1)}, bf16[136,384]{1,0:T(8,128)(2,1)S(1)}) custom-call(s32[4,1]{1,0:T(4,128)} %copy.5.offsets_ref, s32[1]{0:T(128)} %copy.9.step_ref, bf16[136,192]{1,0:T(8,128)(2,1)} %table.1.table_ref, bf16[192,640]{1,0:T(8,128)(2,1)} %bitcast.8), custom_call_target="tpu_custom_call" | custom-call | tf_op jit(solution)/shard_map/unpack/pallas_call | solution.py:245
  17.8 6.6 %conditional.1 = (bf16[136,384]{1,0:T(8,128)(2,1)}) conditional(s32[]{:T(128)} %clamp.3, bf16[136,384]{1,0:T(8,128)(2,1)S(1)} %get-tuple-element.15, bf16[136,384]{1,0:T(8,128)(2,1)S(1)} %get-tuple-element.15, bf16[136,384]{1,0:T(8,128)(2,1)S(1)} %get-tuple-element.15), branch_computations={%region_0.1_spmd, %region_1.2_spmd, %region_2.3_spmd} | conditional | bytes 417840 | solution.py:256
  17.8 1.6 %collective-permute-start.2 = (bf16[136,384]{1,0:T(8,128)(2,1)S(1)}, bf16[136,384]{1,0:T(8,128)(2,1)}, u32[]{:S(2)}, u32[]{:S(2)}) collective-permute-start(bf16[136,384]{1,0:T(8,128)(2,1)S(1)} %param.2), channel_id=1, source_target_pairs={{0,1},{1,2},{2,3},{3,0},{4,5},{5,6},{6,7},{7,4},{8,9},{9,10},{10,1... | collective-permute-start | bytes 313352 | tf_op jit(solution)/shard_map/cond/branch_2_fun/ppermute | solution.py:254
  19.4 5.0 %collective-permute-done.2 = bf16[136,384]{1,0:T(8,128)(2,1)} collective-permute-done((bf16[136,384]{1,0:T(8,128)(2,1)S(1)}, bf16[136,384]{1,0:T(8,128)(2,1)}, u32[]{:S(2)}, u32[]{:S(2)}) %collective-permute-start.2) | collective-permute-done | bytes 104480 | tf_op jit(solution)/shard_map/cond/branch_2_fun/ppermute | solution.py:254
  24.4 0.0 copy-start
  24.4 0.9 %copy-done = bf16[136,256]{1,0:T(8,128)(2,1)S(1)} copy-done((bf16[136,256]{1,0:T(8,128)(2,1)S(1)}, bf16[136,256]{1,0:T(8,128)(2,1)}, u32[]{:S(2)}) %copy-start) | copy-done | bytes 69656
  25.3 17.5 %cost_volume.1 = bf16[128,128,128]{2,1,0:T(8,128)(2,1)} custom-call(bf16[136,256]{1,0:T(8,128)(2,1)S(1)} %copy-done, bf16[136,384]{1,0:T(8,128)(2,1)} %get-tuple-element.16.mate_ref), custom_call_target="tpu_custom_call" | custom-call | tf_op jit(solution)/shard_map/cost_volume/pallas_call | solution.py:134
Async XLA Ops:
  3.2 11.9 %all-to-all-start = ((bf16[8,24,640]{2,1,0:T(8,128)(2,1)}), bf16[8,24,640]{2,1,0:T(8,128)(2,1)S(1)}, u32[]{:S(2)}, u32[]{:S(2)}) async-start(bf16[8,24,640]{2,1,0:T(8,128)(2,1)} %pack.1), calls=%async_computation | async-start | bytes 491520 | tf_op jit(solution)/shard_map/all_to_all | solution.py:239
  15.2 0.7 %copy-start.1 = (bf16[8,24,640]{2,1,0:T(8,128)(2,1)}, bf16[8,24,640]{2,1,0:T(8,128)(2,1)S(1)}, u32[]{:S(2)}) copy-start(bf16[8,24,640]{2,1,0:T(8,128)(2,1)S(1)} %all-to-all-done) | copy-start | bytes 737284
  17.8 6.6 %collective-permute-start.2 = (bf16[136,384]{1,0:T(8,128)(2,1)S(1)}, bf16[136,384]{1,0:T(8,128)(2,1)}, u32[]{:S(2)}, u32[]{:S(2)}) collective-permute-start(bf16[136,384]{1,0:T(8,128)(2,1)S(1)} %param.2), channel_id=1, source_target_pairs={{0,1},{1,2},{2,3},{3,0},{4,5},{5,6},{6,7},{7,4},{8,9},{9,10},{10,1... | collective-permute-start | bytes 313352 | tf_op jit(solution)/shard_map/cond/branch_2_fun/ppermute | solution.py:254
  24.4 0.9 %copy-start = (bf16[136,256]{1,0:T(8,128)(2,1)S(1)}, bf16[136,256]{1,0:T(8,128)(2,1)}, u32[]{:S(2)}) copy-start(bf16[136,256]{1,0:T(8,128)(2,1)} %get-tuple-element.14.ref_ref) | copy-start | bytes 208900

commit v3 on v2

v3 whole, which is shorter than its diff:
```python
import functools

import jax
import jax.numpy as jnp
from jax import lax
from jax.experimental import pallas as pl
from jax.experimental.pallas import tpu as pltpu
from jax.sharding import PartitionSpec as P

COLS = 128
DISP = 128
OFF_MAX = 376


EPSILON = 1e-05


RB = 16
PITCH = 17
PIECES = 2


def box_sums(values, weights):
    f32, bf16 = jnp.float32, jnp.bfloat16
    wide = values.astype(f32)
    square = wide * wide
    high = square.astype(bf16)
    low = (square - high.astype(f32)).astype(bf16)
    total = jnp.dot(values, weights, preferred_element_type=f32)
    total_sq = jnp.dot(high, weights, preferred_element_type=f32)
    return total, total_sq + jnp.dot(low, weights, preferred_element_type=f32)


def cost_kernel(ref_ref, mate_ref, out_ref, ref32, mate32, base, lines_a, lines_b, last_a, last_b, sums, sent, sems,
                mate_sum, mate_sq, ref_sum, ref_sq):
    step = pl.program_id(0)
    rows = ref_ref.shape[0]
    f32, bf16 = jnp.float32, jnp.bfloat16
    down = lax.broadcasted_iota(jnp.int32, (128, 128), 0)
    across = lax.broadcasted_iota(jnp.int32, (128, 128), 1)
    gap = across - down
    band_near = ((gap >= 0) & (gap <= 8)).astype(bf16)
    band_far = ((gap >= -16) & (gap <= -8) & (across >= 112)).astype(bf16)
    lane = lax.broadcasted_iota(jnp.int32, (RB, 128), 1)

    def skew(first, count):
        block = mate32[pl.ds(first, count), :]
        for s in range(16):
            turned = pltpu.roll(block, 1 + s, axis=1)
            for t in range(3):
                for r in range(0, count, 8):
                    base[t, pl.ds(r * PITCH + s, 8, stride=PITCH), :] = turned[r : r + 8, 128 * t : 128 * t + 128]

    def one_line(first, r):
        tiles = [base[t, pl.ds(r * PITCH, 16), :].astype(bf16) for t in range(3)]
        parts = []
        for p in range(-1, 8):
            a, b = divmod(128 - 16 * p, 128)
            if b == 0:
                part = tiles[a]
            else:
                part = pltpu.roll(jnp.where(lane >= b, tiles[a], tiles[a + 1]), 128 - b, axis=1)
            parts.append(part)
        near = jnp.concatenate(parts[1:], axis=0)
        far = jnp.concatenate(parts[:-1], axis=0)
        row = ref32[pl.ds(first + r, 1), :].astype(bf16)
        left = jnp.concatenate([near, far], axis=1)
        right = jnp.concatenate(
            [
                band_near * jnp.broadcast_to(row[:, :128], (128, 128)),
                band_far * jnp.broadcast_to(row[:, 128:], (128, 128)),
            ],
            axis=1,
        )
        return lax.dot_general(left, right, (((1,), (1,)), ((), ())), preferred_element_type=f32)

    @pl.when(step == 0)
    def _():
        ref32[:rows] = ref_ref[...].astype(f32)
        mate32[:rows] = mate_ref[...].astype(f32)
        ref32[rows:] = jnp.zeros((16, 256), f32)
        mate32[rows:] = jnp.zeros((16, 384), f32)
        k = lax.broadcasted_iota(jnp.int32, (384, 256), 0)
        c = lax.broadcasted_iota(jnp.int32, (384, 256), 1)
        total, total_sq = box_sums(mate_ref[...], ((k - c >= 0) & (k - c <= 8)).astype(bf16))
        for t in range(2):
            mate_sum[t] = total[:, 128 * t : 128 * t + 128]
            mate_sq[t] = total_sq[:, 128 * t : 128 * t + 128]
        k = lax.broadcasted_iota(jnp.int32, (256, 128), 0)
        gap_ref = jnp.where(k < 128, k, k - 112) - lax.broadcasted_iota(jnp.int32, (256, 128), 1)
        weights = ((gap_ref >= 0) & (gap_ref <= 8) & ((k < 128) | (k >= 240))).astype(bf16)
        ref_sum[...], ref_sq[...] = box_sums(ref_ref[...], weights)
        skew(0, 8)
        for r in range(8):
            last_a[r] = one_line(0, r)
        skew(8, 16)
        for r in range(16):
            lines_a[r] = one_line(8, r)

    def copy(block, half, piece):
        size = DISP // PIECES
        return pltpu.make_async_copy(
            sent.at[half, pl.ds(piece * size, size)],
            out_ref.at[pl.ds(piece * size, size), pl.ds(pl.multiple_of(block * RB, RB), RB), :],
            sems.at[half, piece],
        )

    def half_step(half, last_in, lines, last_out, lines_next):
        block = 2 * step + half
        first = pl.multiple_of(block * RB, RB)
        ahead = first + RB + 8

        def window(ref):
            x = [ref[pl.ds(first + i, RB), :] for i in range(9)]
            return ((x[0] + x[1]) + (x[2] + x[3])) + ((x[4] + x[5]) + (x[6] + x[7])) + x[8]

        def inverse(total, total_sq):
            mean = total / 81.0
            return lax.rsqrt(jnp.maximum(total_sq / 81.0 - mean * mean, 0.0) + EPSILON)

        total = window(ref_sum)
        ref_mean, ref_inv = total / 81.0, inverse(total, window(ref_sq))
        m0, m1 = window(mate_sum.at[0]), window(mate_sum.at[1])
        v0 = inverse(m0, window(mate_sq.at[0])) / 81.0
        v1 = inverse(m1, window(mate_sq.at[1])) / 81.0

        @pl.when(step > 0)
        def _():
            for piece in range(PIECES):
                copy(block, half, piece).wait()

        skew(pl.multiple_of(ahead, 8), RB)
        for q in range(16):
            lines_next[q] = one_line(ahead, q)
            h = [last_in[i, 8 * q : 8 * q + 8, :] for i in range(8)]
            h += [lines[i, 8 * q : 8 * q + 8, :] for i in range(RB)]
            for i in range(8):
                last_out[i, 8 * q : 8 * q + 8, :] = h[RB + i]
            for begin in range(0, RB, 9):
                suffix = [None] * 8 + [h[begin + 8]]
                for i in range(7, -1, -1):
                    suffix[i] = h[begin + i] + suffix[i + 1]
                prefix = None
                for i in range(min(9, RB - begin)):
                    total = suffix[i]
                    if i:
                        nxt = h[begin + 8 + i]
                        prefix = nxt if prefix is None else prefix + nxt
                        total = total + prefix
                    sums[pl.ds(8 * q * PITCH + begin + i, 8, stride=PITCH), :] = total
            for k in range(8 * q, 8 * q + 8):
                mean, scale = m0, v0
                if k < 127:
                    keep = lane >= 127 - k
                    mean = pltpu.roll(jnp.where(keep, m0, m1), k + 1, axis=1)
                    scale = pltpu.roll(jnp.where(keep, v0, v1), k + 1, axis=1)
                value = (sums[pl.ds(k * PITCH, RB), :] - ref_mean * mean) * ref_inv * scale
                sent[half, k] = value.astype(bf16)
            if (q + 1) % (16 // PIECES) == 0:
                copy(block, half, q // (16 // PIECES)).start()

    half_step(0, last_a, lines_a, last_b, lines_b)
    half_step(1, last_b, lines_b, last_a, lines_a)

    @pl.when(step == pl.num_programs(0) - 1)
    def _():
        for half in range(2):
            for piece in range(PIECES):
                copy(0, half, piece).wait()


def cost(ref_rows, mate_rows):
    rows = ref_rows.shape[0]
    f32 = jnp.float32
    vmem = pl.BlockSpec(memory_space=pltpu.VMEM)
    return pl.pallas_call(
        cost_kernel,
        out_shape=jax.ShapeDtypeStruct((DISP, rows - 8, COLS), jnp.bfloat16),
        grid=((rows - 8) // (2 * RB),),
        in_specs=[vmem, vmem],
        out_specs=pl.BlockSpec(memory_space=pl.ANY),
        scratch_shapes=[
            pltpu.VMEM((rows + 16, 256), f32),
            pltpu.VMEM((rows + 16, 384), f32),
            pltpu.VMEM((3, 16 * PITCH + 8, 128), f32),
            pltpu.VMEM((RB, 128, 128), f32),
            pltpu.VMEM((RB, 128, 128), f32),
            pltpu.VMEM((8, 128, 128), f32),
            pltpu.VMEM((8, 128, 128), f32),
            pltpu.VMEM((128 * PITCH + 8, 128), f32),
            pltpu.VMEM((2, DISP, RB, COLS), jnp.bfloat16),
            pltpu.SemaphoreType.DMA((2, PIECES)),
            pltpu.VMEM((2, rows, 128), f32),
            pltpu.VMEM((2, rows, 128), f32),
            pltpu.VMEM((rows, 128), f32),
            pltpu.VMEM((rows, 128), f32),
        ],
        compiler_params=pltpu.CompilerParams(dimension_semantics=("arbitrary",), vmem_limit_bytes=40 << 20),
        name="cost_volume",
    )(ref_rows, mate_rows)


SPAN = COLS + DISP + 8
EDGE = 4
REF_FROM = OFF_MAX + DISP - 1


def slot_count(rows_dev, strips):
    wide = rows_dev // strips + 2 * EDGE
    return -(-wide // 8) * 8


def places(ids, low, rows_dev):
    line = ids.shape[1]
    place = ids - low + EDGE
    wanted = (place >= 0) & (place < rows_dev + 2 * EDGE)
    before = lax.broadcasted_iota(jnp.int32, (line, line), 0)
    after = lax.broadcasted_iota(jnp.int32, (line, line), 1)
    earlier = (before < after).astype(jnp.bfloat16)
    flags = jnp.where(wanted, 1.0, 0.0)
    pad = (-flags.shape[0]) % 16
    if pad:
        flags = jnp.concatenate([flags, jnp.zeros((pad, line), jnp.float32)], axis=0)
    rank = jnp.dot(flags.astype(jnp.bfloat16), earlier, preferred_element_type=jnp.float32)
    rank = rank[: ids.shape[0]].astype(jnp.int32)
    return jnp.where(wanted, rank, -1), place


def spread(rank, slots):
    strips, line = rank.shape
    wide = jnp.broadcast_to(rank[:, None, :], (strips, slots, line))
    return wide == lax.broadcasted_iota(jnp.int32, (strips, slots, line), 1)


def pack_kernel(map_ref, tiles_ref, out_ref):
    strips, slots, width = out_ref.shape
    rows_dev = tiles_ref.shape[0]
    ids = jnp.broadcast_to(map_ref[pl.ds(lax.axis_index("strip"), 1), :], (strips, rows_dev))
    low = rows_dev * lax.broadcasted_iota(jnp.int32, (strips, rows_dev), 0)
    rank, _ = places(ids, low, rows_dev)
    pick = jnp.where(spread(rank, slots), 1.0, 0.0).reshape(strips * slots, rows_dev).astype(jnp.bfloat16)
    rows = jnp.dot(pick, tiles_ref[...], preferred_element_type=jnp.float32)
    out_ref[...] = rows.astype(jnp.bfloat16).reshape(out_ref.shape)


def table_kernel(table_ref, out_ref):
    strips, rows_dev = table_ref.shape
    rows, positions = out_ref.shape
    slots = positions // strips
    low = rows_dev * lax.axis_index("strip")
    rank, place = places(table_ref[...], low, rows_dev)
    wide = jnp.broadcast_to(place[:, None, :], (strips, slots, rows_dev))
    named = jnp.where(spread(rank, slots), wide + 1, 0).astype(jnp.float32)
    named = named.reshape(positions, rows_dev).astype(jnp.bfloat16)
    ones = jnp.ones((16, rows_dev), jnp.bfloat16)
    target = lax.dot_general(ones, named, (((1,), (1,)), ((), ())), preferred_element_type=jnp.float32)
    target = jnp.broadcast_to(target[:1].astype(jnp.int32), (rows, positions))
    mine = lax.broadcasted_iota(jnp.int32, (rows, positions), 0) + 1
    out_ref[...] = jnp.where(target == mine, 1.0, 0.0).astype(jnp.bfloat16)


def unpack_kernel(offsets_ref, step_ref, table_ref, arrived_ref, ref_ref, slab_ref, strip):
    rows = ref_ref.shape[0]
    width = arrived_ref.shape[1]
    views = offsets_ref.shape[0]
    own = jnp.dot(table_ref[...], arrived_ref[...], preferred_element_type=jnp.float32)
    strip[:, :width] = own
    strip[:, width:] = jnp.zeros((rows, strip.shape[1] - width), jnp.float32)
    ref_ref[:, :128] = own[:, REF_FROM : REF_FROM + 128].astype(jnp.bfloat16)
    ref_ref[:, 128:] = strip[:, REF_FROM + 16 : REF_FROM + 144].astype(jnp.bfloat16)
    receiver = lax.rem(lax.axis_index("view") + views - lax.rem(step_ref[0], views), views)
    start = jnp.clip(OFF_MAX - offsets_ref[receiver, 0], 0, OFF_MAX)
    whole = start // 128
    part = start - whole * 128
    block = strip[:, pl.ds(pl.multiple_of(whole * 128, 128), 512)]
    turned = pltpu.roll(block, 512 - part, axis=1)
    slab_ref[...] = turned[:, :384].astype(jnp.bfloat16)


def shards(images, offsets, pair_step, row_map):
    own_tiles = images[0]
    rows_dev, width = own_tiles.shape
    strips = lax.axis_size("strip")
    views = lax.axis_size("view")
    slots = slot_count(rows_dev, strips)
    rows = rows_dev + 2 * EDGE
    bf16 = jnp.bfloat16
    table = row_map.reshape(strips, rows_dev)
    outgoing = pl.pallas_call(
        pack_kernel, out_shape=jax.ShapeDtypeStruct((strips, slots, width), bf16), name="pack"
    )(table, own_tiles)
    arrived = lax.all_to_all(outgoing, "strip", split_axis=0, concat_axis=0, tiled=True)
    select = pl.pallas_call(
        table_kernel, out_shape=jax.ShapeDtypeStruct((rows, strips * slots), bf16), name="table"
    )(table)
    smem = pl.BlockSpec(memory_space=pltpu.SMEM)
    vmem = pl.BlockSpec(memory_space=pltpu.VMEM)
    ref_rows, slab = pl.pallas_call(
        unpack_kernel,
        out_shape=(jax.ShapeDtypeStruct((rows, 256), bf16), jax.ShapeDtypeStruct((rows, 384), bf16)),
        in_specs=[smem, smem, vmem, vmem],
        scratch_shapes=[pltpu.VMEM((rows, 768), jnp.float32)],
        name="unpack",
    )(offsets, pair_step, select, arrived.reshape(strips * slots, width))

    def sent_by(step):
        return lambda rows_out: lax.ppermute(rows_out, "view", [(i, (i - step) % views) for i in range(views)])

    mate_rows = lax.switch(pair_step[0] % views - 1, [sent_by(step) for step in range(1, views)], slab)
    return cost(ref_rows, mate_rows)[None]


def solution(mesh):
    in_specs = (P("view", "strip", None), P(None, "strip"), P("strip"), P())
    out_specs = P("view", None, "strip", None)
    return jax.shard_map(shards, mesh=mesh, in_specs=in_specs, out_specs=out_specs, check_vma=False)
```

time: 43.2 us -> 35.1 us (0.81); the launches traced: 42.8 us -> 35.4 us
  Pallas kernels: 23 us -> 16.3 us
  local copies, waits for them, and re-layouts: 4.14 us -> 2.87 us
  starting transfers between devices: 6.75 us -> 7.76 us
    pallas_call x1, Pallas kernels: 17.5 us -> 10.8 us  [cost(): pl.pallas_call(cost_kernel, out_shape=jax.ShapeDtypeStruct((DISP, rows -...]
    dynamic_slice x1 -> x0, local copies, waits for them, and re-layouts: 1.27 us -> none  [shards(): local = lax.dynamic_slice_in_dim(table, strip_me, 1)]
    ppermute x1, starting transfers between devices: 1.58 us -> 2.59 us  [sent_by(): lax.ppermute(rows_out, 'view', [(i, (i - step) % views) for i in range(vi...]
  transfers between devices with their start and end apart: 2 -> 2, of which waited for: 2 -> 2; matrix products, arithmetic and copies ran while one was open for 3% -> 4% of each run, Pallas kernels for 4% -> 5%
where the time goes in v3:
time: 35.1 us; the launch traced here: 35.4 us
  Pallas kernels  16.3 us (46%)
  starting transfers between devices  7.76 us (22%)
  waiting for transfers between devices  7.76 us (22%)
  local copies, waits for them, and re-layouts  2.87 us (8%)
  between operations  0.67 us (2%)
    pallas_call x1, Pallas kernels, cost(): pl.pallas_call(cost_kernel, out_shape=jax.ShapeDtypeStruct((DISP, rows -...  10.8 us
    all_to_all x1, starting transfers between devices, shards(): lax.all_to_all(outgoing, 'strip', split_axis=0, concat_axis=0, tiled=True)  5.17 us
    ppermute x1, waiting for transfers between devices, sent_by(): lax.ppermute(rows_out, 'view', [(i, (i - step) % views) for i in range(vi...  4.6 us
    all_to_all x1, waiting for transfers between devices, shards(): lax.all_to_all(outgoing, 'strip', split_axis=0, concat_axis=0, tiled=True)  3.16 us
    unnamed x5, local copies, waits for them, and re-layouts  2.87 us
    ppermute x1, starting transfers between devices, sent_by(): lax.ppermute(rows_out, 'view', [(i, (i - step) % views) for i in range(vi...  2.59 us
    pallas_call x1, Pallas kernels, shards(): pl.pallas_call(pack_kernel, out_shape=jax.ShapeDtypeStruct((strips, slots...  1.96 us
    pallas_call x1, Pallas kernels, shards(): pl.pallas_call(unpack_kernel, out_shape=(jax.ShapeDtypeStruct((rows, 256)...  1.95 us
  transfers between devices with their start and end apart: 2, of which 2 were waited for; matrix products, arithmetic and copies ran while one was open for 4% of the time, Pallas kernels for 5%

profile of v3, /device:TPU:0, one launch (start us, length us, event | category | flops | bytes accessed | tf_op | source)
XLA Modules:
  0.0 35.4 jit_solution(7681571217075849972)
XLA Ops:
  0.0 2.0 %pack.1 = bf16[8,24,640]{2,1,0:T(8,128)(2,1)} custom-call(s32[8,128]{1,0:T(8,128)} %bitcast.10, bf16[128,640]{1,0:T(8,128)(2,1)} %bitcast.9), custom_call_target="tpu_custom_call" | custom-call | tf_op jit(solution)/shard_map/pack/pallas_call | solution.py:289
  2.0 5.2 %all-to-all-start = ((bf16[8,24,640]{2,1,0:T(8,128)(2,1)}), bf16[8,24,640]{2,1,0:T(8,128)(2,1)S(1)}, u32[]{:S(2)}, u32[]{:S(2)}) async-start(bf16[8,24,640]{2,1,0:T(8,128)(2,1)} %pack.1), calls=%async_computation | async-start | bytes 491520 | tf_op jit(solution)/shard_map/all_to_all | solution.py:292
  7.8 1.6 %table.1.table_ref = bf16[136,192]{1,0:T(8,128)(2,1)} custom-call(s32[8,128]{1,0:T(8,128)} %bitcast.11), custom_call_target="tpu_custom_call" | custom-call | tf_op jit(solution)/shard_map/table/pallas_call | solution.py:293
  9.4 1.3 %copy.5.offsets_ref = s32[4,1]{1,0:T(4,128)} copy(s32[4,1]{0,1:T(1,128)} %param.8) | data formatting | bytes 32 | tf_op args[1]
  10.7 3.2 %all-to-all-done = bf16[8,24,640]{2,1,0:T(8,128)(2,1)S(1)} async-done(((bf16[8,24,640]{2,1,0:T(8,128)(2,1)}), bf16[8,24,640]{2,1,0:T(8,128)(2,1)S(1)}, u32[]{:S(2)}, u32[]{:S(2)}) %all-to-all-start) | async-done | bytes 245792 | tf_op jit(solution)/shard_map/all_to_all | solution.py:292
  13.9 0.0 copy-start.1
  13.9 0.7 %copy-done.1 = bf16[8,24,640]{2,1,0:T(8,128)(2,1)} copy-done((bf16[8,24,640]{2,1,0:T(8,128)(2,1)}, bf16[8,24,640]{2,1,0:T(8,128)(2,1)S(1)}, u32[]{:S(2)}) %copy-start.1) | copy-done | bytes 245784
  14.6 2.0 %unpack.1 = (bf16[136,256]{1,0:T(8,128)(2,1)}, bf16[136,384]{1,0:T(8,128)(2,1)S(1)}) custom-call(s32[4,1]{1,0:T(4,128)} %copy.5.offsets_ref, s32[1]{0:T(128)} %copy.9.step_ref, bf16[136,192]{1,0:T(8,128)(2,1)} %table.1.table_ref, bf16[192,640]{1,0:T(8,128)(2,1)} %bitcast.8), custom_call_target="tpu_custom_call" | custom-call | tf_op jit(solution)/shard_map/unpack/pallas_call | solution.py:298
  16.5 7.2 %conditional.1 = (bf16[136,384]{1,0:T(8,128)(2,1)}) conditional(s32[]{:T(128)} %clamp.3, bf16[136,384]{1,0:T(8,128)(2,1)S(1)} %get-tuple-element.15, bf16[136,384]{1,0:T(8,128)(2,1)S(1)} %get-tuple-element.15, bf16[136,384]{1,0:T(8,128)(2,1)S(1)} %get-tuple-element.15), branch_computations={%region_0.1_spmd, %region_1.2_spmd, %region_2.3_spmd} | conditional | bytes 417840 | solution.py:309
  16.5 2.6 %collective-permute-start.1 = (bf16[136,384]{1,0:T(8,128)(2,1)S(1)}, bf16[136,384]{1,0:T(8,128)(2,1)}, u32[]{:S(2)}, u32[]{:S(2)}) collective-permute-start(bf16[136,384]{1,0:T(8,128)(2,1)S(1)} %param.1), channel_id=1, source_target_pairs={{0,2},{1,3},{2,0},{3,1},{4,6},{5,7},{6,4},{7,5},{8,10},{9,11},{10,... | collective-permute-start | bytes 313352 | tf_op jit(solution)/shard_map/cond/branch_1_fun/ppermute | solution.py:307
  19.1 4.6 %collective-permute-done.1 = bf16[136,384]{1,0:T(8,128)(2,1)} collective-permute-done((bf16[136,384]{1,0:T(8,128)(2,1)S(1)}, bf16[136,384]{1,0:T(8,128)(2,1)}, u32[]{:S(2)}, u32[]{:S(2)}) %collective-permute-start.1) | collective-permute-done | bytes 104480 | tf_op jit(solution)/shard_map/cond/branch_1_fun/ppermute | solution.py:307
  23.7 0.0 copy-start
  23.7 0.9 %copy-done = bf16[136,256]{1,0:T(8,128)(2,1)S(1)} copy-done((bf16[136,256]{1,0:T(8,128)(2,1)S(1)}, bf16[136,256]{1,0:T(8,128)(2,1)}, u32[]{:S(2)}) %copy-start) | copy-done | bytes 69656
  24.6 10.8 %cost_volume.1 = bf16[128,128,128]{2,1,0:T(8,128)(2,1)} custom-call(bf16[136,256]{1,0:T(8,128)(2,1)S(1)} %copy-done, bf16[136,384]{1,0:T(8,128)(2,1)} %get-tuple-element.16.mate_ref), custom_call_target="tpu_custom_call" | custom-call | tf_op jit(solution)/shard_map/cost_volume/pallas_call | solution.py:176
Async XLA Ops:
  2.0 11.9 %all-to-all-start = ((bf16[8,24,640]{2,1,0:T(8,128)(2,1)}), bf16[8,24,640]{2,1,0:T(8,128)(2,1)S(1)}, u32[]{:S(2)}, u32[]{:S(2)}) async-start(bf16[8,24,640]{2,1,0:T(8,128)(2,1)} %pack.1), calls=%async_computation | async-start | bytes 491520 | tf_op jit(solution)/shard_map/all_to_all | solution.py:292
  13.9 0.7 %copy-start.1 = (bf16[8,24,640]{2,1,0:T(8,128)(2,1)}, bf16[8,24,640]{2,1,0:T(8,128)(2,1)S(1)}, u32[]{:S(2)}) copy-start(bf16[8,24,640]{2,1,0:T(8,128)(2,1)S(1)} %all-to-all-done) | copy-start | bytes 737284
  16.5 7.2 %collective-permute-start.1 = (bf16[136,384]{1,0:T(8,128)(2,1)S(1)}, bf16[136,384]{1,0:T(8,128)(2,1)}, u32[]{:S(2)}, u32[]{:S(2)}) collective-permute-start(bf16[136,384]{1,0:T(8,128)(2,1)S(1)} %param.1), channel_id=1, source_target_pairs={{0,2},{1,3},{2,0},{3,1},{4,6},{5,7},{6,4},{7,5},{8,10},{9,11},{10,... | collective-permute-start | bytes 313352 | tf_op jit(solution)/shard_map/cond/branch_1_fun/ppermute | solution.py:307
  23.7 0.9 %copy-start = (bf16[136,256]{1,0:T(8,128)(2,1)S(1)}, bf16[136,256]{1,0:T(8,128)(2,1)}, u32[]{:S(2)}) copy-start(bf16[136,256]{1,0:T(8,128)(2,1)} %get-tuple-element.14.ref_ref) | copy-start | bytes 208900

commit v4 on v3

--- a/solution.py
+++ b/solution.py
@@ -31,8 +31,8 @@
     return total, total_sq + jnp.dot(low, weights, preferred_element_type=f32)
 
 
-def cost_kernel(ref_ref, mate_ref, out_ref, ref32, mate32, base, lines_a, lines_b, last_a, last_b, sums, sent, sems,
-                mate_sum, mate_sq, ref_sum, ref_sq):
+def cost_kernel(ref_ref, mate_ref, out_ref, ref32, mate32, base_a, base_b, lines_a, lines_b, last_a, last_b, sums_a, sums_b, sent, sems,
+                mate_sum, mate_sq, ref_sum, ref_sq, stats):
     step = pl.program_id(0)
     rows = ref_ref.shape[0]
     f32, bf16 = jnp.float32, jnp.bfloat16
@@ -40,38 +40,42 @@
     across = lax.broadcasted_iota(jnp.int32, (128, 128), 1)
     gap = across - down
     band_near = ((gap >= 0) & (gap <= 8)).astype(bf16)
-    band_far = ((gap >= -16) & (gap <= -8) & (across >= 112)).astype(bf16)
-    lane = lax.broadcasted_iota(jnp.int32, (RB, 128), 1)
-
-    def skew(first, count):
-        block = mate32[pl.ds(first, count), :]
-        for s in range(16):
-            turned = pltpu.roll(block, 1 + s, axis=1)
-            for t in range(3):
-                for r in range(0, count, 8):
-                    base[t, pl.ds(r * PITCH + s, 8, stride=PITCH), :] = turned[r : r + 8, 128 * t : 128 * t + 128]
-
-    def one_line(first, r):
-        tiles = [base[t, pl.ds(r * PITCH, 16), :].astype(bf16) for t in range(3)]
+    band_far = ((gap >= -16) & (gap <= -8) & (across >= 112)).astype(bf16)[112:]
+    lane = lax.broadcasted_iota(jnp.int32, (8, 128), 1)
+    lane_two = lax.broadcasted_iota(jnp.int32, (16, 128), 1)
+
+    def skew(base, block, s):
+        shift = 15 - s
+        for t in range(2):
+            part = block[t]
+            if shift:
+                part = pltpu.roll(jnp.where(lane_two < shift, block[t + 1], part), 128 - shift, axis=1)
+            part = part.astype(f32)
+            for r in range(0, RB, 8):
+                base[t, pl.ds(r * PITCH + s, 8, stride=PITCH), :] = part[r : r + 8]
+
+    def lines_from(first):
+        block = mate32[pl.ds(first, RB), :].astype(bf16)
+        return [block[:, 128 * t : 128 * t + 128] for t in range(3)]
+
+    def one_line(base, first, r):
+        tiles = [base[t, pl.ds(r * PITCH, 16), :].astype(bf16) for t in range(2)]
         parts = []
         for p in range(-1, 8):
-            a, b = divmod(128 - 16 * p, 128)
-            if b == 0:
-                part = tiles[a]
+            shift = 112 - 16 * p
+            if shift in (0, 128):
+                part = tiles[shift // 128]
             else:
-                part = pltpu.roll(jnp.where(lane >= b, tiles[a], tiles[a + 1]), 128 - b, axis=1)
+                part = pltpu.roll(jnp.where(lane_two < shift, tiles[1], tiles[0]), 128 - shift, axis=1)
             parts.append(part)
         near = jnp.concatenate(parts[1:], axis=0)
         far = jnp.concatenate(parts[:-1], axis=0)
         row = ref32[pl.ds(first + r, 1), :].astype(bf16)
         left = jnp.concatenate([near, far], axis=1)
-        right = jnp.concatenate(
-            [
-                band_near * jnp.broadcast_to(row[:, :128], (128, 128)),
-                band_far * jnp.broadcast_to(row[:, 128:], (128, 128)),
-            ],
-            axis=1,
+        beyond = jnp.concatenate(
+            [jnp.zeros((112, 128), bf16), band_far * jnp.broadcast_to(row[:, 128:], (16, 128))], axis=0
         )
+        right = jnp.concatenate([band_near * jnp.broadcast_to(row[:, :128], (128, 128)), beyond], axis=1)
         return lax.dot_general(left, right, (((1,), (1,)), ((), ())), preferred_element_type=f32)
 
     @pl.when(step == 0)
@@ -79,7 +83,7 @@
         ref32[:rows] = ref_ref[...].astype(f32)
         mate32[:rows] = mate_ref[...].astype(f32)
         ref32[rows:] = jnp.zeros((16, 256), f32)
-        mate32[rows:] = jnp.zeros((16, 384), f32)
+        mate32[rows:] = jnp.zeros((32, 384), f32)
         k = lax.broadcasted_iota(jnp.int32, (384, 256), 0)
         c = lax.broadcasted_iota(jnp.int32, (384, 256), 1)
         total, total_sq = box_sums(mate_ref[...], ((k - c >= 0) & (k - c <= 8)).astype(bf16))
@@ -90,12 +94,33 @@
         gap_ref = jnp.where(k < 128, k, k - 112) - lax.broadcasted_iota(jnp.int32, (256, 128), 1)
         weights = ((gap_ref >= 0) & (gap_ref <= 8) & ((k < 128) | (k >= 240))).astype(bf16)
         ref_sum[...], ref_sq[...] = box_sums(ref_ref[...], weights)
-        skew(0, 8)
+        for base, first in ((base_b, 0), (base_a, 8)):
+            block = lines_from(first)
+            for s in range(16):
+                skew(base, block, s)
         for r in range(8):
-            last_a[r] = one_line(0, r)
-        skew(8, 16)
+            last_a[r] = one_line(base_b, 0, r)
         for r in range(16):
-            lines_a[r] = one_line(8, r)
+            lines_a[r] = one_line(base_a, 8, r)
+        block = lines_from(24)
+        for s in range(16):
+            skew(base_b, block, s)
+
+        def window(ref):
+            x = [ref[i : i + rows - 8, :] for i in range(9)]
+            return ((x[0] + x[1]) + (x[2] + x[3])) + ((x[4] + x[5]) + (x[6] + x[7])) + x[8]
+
+        def inverse(total, total_sq):
+            mean = total / 81.0
+            return lax.rsqrt(jnp.maximum(total_sq / 81.0 - mean * mean, 0.0) + EPSILON)
+
+        for t in range(2):
+            total = window(mate_sum.at[t])
+            stats[t] = total
+            stats[2 + t] = inverse(total, window(mate_sq.at[t])) / 81.0
+        total = window(ref_sum)
+        stats[4] = total / 81.0
+        stats[5] = inverse(total, window(ref_sq))
 
     def copy(block, half, piece):
         size = DISP // PIECES
@@ -105,33 +130,19 @@
             sems.at[half, piece],
         )
 
-    def half_step(half, last_in, lines, last_out, lines_next):
+    def half_step(half, last_in, lines, last_out, lines_next, base, base_next):
         block = 2 * step + half
         first = pl.multiple_of(block * RB, RB)
         ahead = first + RB + 8
-
-        def window(ref):
-            x = [ref[pl.ds(first + i, RB), :] for i in range(9)]
-            return ((x[0] + x[1]) + (x[2] + x[3])) + ((x[4] + x[5]) + (x[6] + x[7])) + x[8]
-
-        def inverse(total, total_sq):
-            mean = total / 81.0
-            return lax.rsqrt(jnp.maximum(total_sq / 81.0 - mean * mean, 0.0) + EPSILON)
-
-        total = window(ref_sum)
-        ref_mean, ref_inv = total / 81.0, inverse(total, window(ref_sq))
-        m0, m1 = window(mate_sum.at[0]), window(mate_sum.at[1])
-        v0 = inverse(m0, window(mate_sq.at[0])) / 81.0
-        v1 = inverse(m1, window(mate_sq.at[1])) / 81.0
 
         @pl.when(step > 0)
         def _():
             for piece in range(PIECES):
                 copy(block, half, piece).wait()
 
-        skew(pl.multiple_of(ahead, 8), RB)
-        for q in range(16):
-            lines_next[q] = one_line(ahead, q)
+        block_next = lines_from(pl.multiple_of(ahead + RB, 8))
+
+        def vertical(q, sums):
             h = [last_in[i, 8 * q : 8 * q + 8, :] for i in range(8)]
             h += [lines[i, 8 * q : 8 * q + 8, :] for i in range(RB)]
             for i in range(8):
@@ -147,20 +158,37 @@
                         nxt = h[begin + 8 + i]
                         prefix = nxt if prefix is None else prefix + nxt
                         total = total + prefix
-                    sums[pl.ds(8 * q * PITCH + begin + i, 8, stride=PITCH), :] = total
-            for k in range(8 * q, 8 * q + 8):
-                mean, scale = m0, v0
-                if k < 127:
-                    keep = lane >= 127 - k
-                    mean = pltpu.roll(jnp.where(keep, m0, m1), k + 1, axis=1)
-                    scale = pltpu.roll(jnp.where(keep, v0, v1), k + 1, axis=1)
-                value = (sums[pl.ds(k * PITCH, RB), :] - ref_mean * mean) * ref_inv * scale
-                sent[half, k] = value.astype(bf16)
+                    sums[pl.ds(begin + i, 8, stride=PITCH), :] = total
+
+        def normalize(q, sums):
+            for j in range(8):
+                k = 8 * q + j
+                done = []
+                for u in range(0, RB, 8):
+                    m0, m1, v0, v1, ref_mean, ref_inv = [
+                        stats[i, pl.ds(pl.multiple_of(first + u, 8), 8), :] for i in range(6)
+                    ]
+                    mean, scale = m0, v0
+                    if k < 127:
+                        mean = pltpu.roll(jnp.where(lane >= 127 - k, m0, m1), k + 1, axis=1)
+                        scale = pltpu.roll(jnp.where(lane >= 127 - k, v0, v1), k + 1, axis=1)
+                    total = sums[pl.ds(j * PITCH + u, 8), :]
+                    done.append((total - ref_mean * mean) * ref_inv * scale)
+                sent[half, k] = jnp.concatenate(done, axis=0).astype(bf16)
             if (q + 1) % (16 // PIECES) == 0:
                 copy(block, half, q // (16 // PIECES)).start()
 
-    half_step(0, last_a, lines_a, last_b, lines_b)
-    half_step(1, last_b, lines_b, last_a, lines_a)
+        both = (sums_a, sums_b)
+        for q in range(16):
+            lines_next[q] = one_line(base, ahead, q)
+            skew(base_next, block_next, q)
+            vertical(q, both[q % 2])
+            if q:
+                normalize(q - 1, both[(q - 1) % 2])
+        normalize(15, both[1])
+
+    half_step(0, last_a, lines_a, last_b, lines_b, base_b, base_a)
+    half_step(1, last_b, lines_b, last_a, lines_a, base_a, base_b)
 
     @pl.when(step == pl.num_programs(0) - 1)
     def _():
@@ -181,27 +209,31 @@
         out_specs=pl.BlockSpec(memory_space=pl.ANY),
         scratch_shapes=[
             pltpu.VMEM((rows + 16, 256), f32),
-            pltpu.VMEM((rows + 16, 384), f32),
-            pltpu.VMEM((3, 16 * PITCH + 8, 128), f32),
+            pltpu.VMEM((rows + 32, 384), f32),
+            pltpu.VMEM((2, 16 * PITCH + 8, 128), f32),
+            pltpu.VMEM((2, 16 * PITCH + 8, 128), f32),
             pltpu.VMEM((RB, 128, 128), f32),
             pltpu.VMEM((RB, 128, 128), f32),
             pltpu.VMEM((8, 128, 128), f32),
             pltpu.VMEM((8, 128, 128), f32),
-            pltpu.VMEM((128 * PITCH + 8, 128), f32),
+            pltpu.VMEM((8 * PITCH + 8, 128), f32),
+            pltpu.VMEM((8 * PITCH + 8, 128), f32),
             pltpu.VMEM((2, DISP, RB, COLS), jnp.bfloat16),
             pltpu.SemaphoreType.DMA((2, PIECES)),
             pltpu.VMEM((2, rows, 128), f32),
             pltpu.VMEM((2, rows, 128), f32),
             pltpu.VMEM((rows, 128), f32),
             pltpu.VMEM((rows, 128), f32),
+            pltpu.VMEM((6, rows - 8, 128), f32),
         ],
-        compiler_params=pltpu.CompilerParams(dimension_semantics=("arbitrary",), vmem_limit_bytes=40 << 20),
+        compiler_params=pltpu.CompilerParams(dimension_semantics=("arbitrary",), vmem_limit_bytes=16 << 20),
         name="cost_volume",
     )(ref_rows, mate_rows)
 
 
 SPAN = COLS + DISP + 8
 EDGE = 4
+SMALL = pltpu.CompilerParams(vmem_limit_bytes=16 << 20)
 REF_FROM = OFF_MAX + DISP - 1
 
 
@@ -291,7 +323,7 @@
     )(table, own_tiles)
     arrived = lax.all_to_all(outgoing, "strip", split_axis=0, concat_axis=0, tiled=True)
     select = pl.pallas_call(
-        table_kernel, out_shape=jax.ShapeDtypeStruct((rows, strips * slots), bf16), name="table"
+        table_kernel, out_shape=jax.ShapeDtypeStruct((rows, strips * slots), bf16), name="table", compiler_params=SMALL
     )(table)
     smem = pl.BlockSpec(memory_space=pltpu.SMEM)
     vmem = pl.BlockSpec(memory_space=pltpu.VMEM)
@@ -300,6 +332,7 @@
         out_shape=(jax.ShapeDtypeStruct((rows, 256), bf16), jax.ShapeDtypeStruct((rows, 384), bf16)),
         in_specs=[smem, smem, vmem, vmem],
         scratch_shapes=[pltpu.VMEM((rows, 768), jnp.float32)],
+        compiler_params=SMALL,
         name="unpack",
     )(offsets, pair_step, select, arrived.reshape(strips * slots, width))
 

time: 35.1 us -> 30.8 us (0.88); the launches traced: 35.4 us -> 30.5 us
  Pallas kernels: 16.3 us -> 12.9 us
  local copies, waits for them, and re-layouts: 2.87 us -> 1.43 us
  waiting for transfers between devices: 7.76 us -> 6.64 us
  starting transfers between devices: 7.76 us -> 8.83 us
    ppermute x1, waiting for transfers between devices: 4.6 us -> 2.3 us  [sent_by(): lax.ppermute(rows_out, 'view', [(i, (i - step) % views) for i in range(vi...]
    unnamed x5 -> x3, local copies, waits for them, and re-layouts: 2.87 us -> 1.43 us
    pallas_call x1, Pallas kernels: 1.64 us -> 0.32 us  [shards(): pl.pallas_call(table_kernel, out_shape=jax.ShapeDtypeStruct((rows, strips...]
    all_to_all x1, waiting for transfers between devices: 3.16 us -> 4.34 us  [shards(): lax.all_to_all(outgoing, 'strip', split_axis=0, concat_axis=0, tiled=True)]
    ppermute x1, starting transfers between devices: 2.59 us -> 3.66 us  [sent_by(): lax.ppermute(rows_out, 'view', [(i, (i - step) % views) for i in range(vi...]
    pallas_call x1, Pallas kernels: 10.8 us -> 9.72 us  [cost(): pl.pallas_call(cost_kernel, out_shape=jax.ShapeDtypeStruct((DISP, rows -...]
    pallas_call x1, Pallas kernels: 1.95 us -> 0.92 us  [shards(): pl.pallas_call(unpack_kernel, out_shape=(jax.ShapeDtypeStruct((rows, 256)...]
  transfers between devices with their start and end apart: 2 -> 2, of which waited for: 2 -> 2; matrix products, arithmetic and copies ran while one was open for 4% -> 2% of each run, Pallas kernels for 5% -> 1%
where the time goes in v4:
time: 30.8 us; the launch traced here: 30.5 us
  Pallas kernels  12.9 us (42%)
  starting transfers between devices  8.83 us (29%)
  waiting for transfers between devices  6.64 us (22%)
  local copies, waits for them, and re-layouts  1.43 us (5%)
  between operations  0.69 us (2%)
    pallas_call x1, Pallas kernels, cost(): pl.pallas_call(cost_kernel, out_shape=jax.ShapeDtypeStruct((DISP, rows -...  9.72 us
    all_to_all x1, starting transfers between devices, shards(): lax.all_to_all(outgoing, 'strip', split_axis=0, concat_axis=0, tiled=True)  5.17 us
    all_to_all x1, waiting for transfers between devices, shards(): lax.all_to_all(outgoing, 'strip', split_axis=0, concat_axis=0, tiled=True)  4.34 us
    ppermute x1, starting transfers between devices, sent_by(): lax.ppermute(rows_out, 'view', [(i, (i - step) % views) for i in range(vi...  3.66 us
    ppermute x1, waiting for transfers between devices, sent_by(): lax.ppermute(rows_out, 'view', [(i, (i - step) % views) for i in range(vi...  2.3 us
    pallas_call x1, Pallas kernels, shards(): pl.pallas_call(pack_kernel, out_shape=jax.ShapeDtypeStruct((strips, slots...  1.96 us
    unnamed x3, local copies, waits for them, and re-layouts  1.43 us
    pallas_call x1, Pallas kernels, shards(): pl.pallas_call(unpack_kernel, out_shape=(jax.ShapeDtypeStruct((rows, 256)...  0.92 us
  transfers between devices with their start and end apart: 2, of which 2 were waited for; matrix products, arithmetic and copies ran while one was open for 2% of the time, Pallas kernels for 1%

profile of v4, /device:TPU:0, one launch (start us, length us, event | category | flops | bytes accessed | tf_op | source)
XLA Modules:
  0.0 30.5 jit_solution(6141444453322607028)
XLA Ops:
  0.0 2.0 %pack.1 = bf16[8,24,640]{2,1,0:T(8,128)(2,1)} custom-call(s32[8,128]{1,0:T(8,128)} %bitcast.9, bf16[128,640]{1,0:T(8,128)(2,1)} %bitcast.11), custom_call_target="tpu_custom_call" | custom-call | tf_op jit(solution)/shard_map/pack/pallas_call | solution.py:321
  2.0 5.2 %all-to-all-start = ((bf16[8,24,640]{2,1,0:T(8,128)(2,1)}), bf16[8,24,640]{2,1,0:T(8,128)(2,1)S(1)}, u32[]{:S(2)}, u32[]{:S(2)}) async-start(bf16[8,24,640]{2,1,0:T(8,128)(2,1)} %pack.1), calls=%async_computation | async-start | bytes 491520 | tf_op jit(solution)/shard_map/all_to_all | solution.py:324
  7.8 0.0 copy-start
  7.8 0.7 %copy-done = s32[1024]{0:T(1024)S(1)} copy-done((s32[1024]{0:T(1024)S(1)}, s32[1024]{0:T(1024)}, u32[]{:S(2)}) %copy-start) | copy-done | bytes 4120
  8.5 0.3 %table.1.table_ref = bf16[136,192]{1,0:T(8,128)(2,1)S(1)} custom-call(s32[8,128]{1,0:T(8,128)S(1)} %bitcast.10), custom_call_target="tpu_custom_call" | custom-call | tf_op jit(solution)/shard_map/table/pallas_call | solution.py:325
  8.8 0.7 %copy.5.offsets_ref = s32[4,1]{1,0:T(4,128)S(1)} copy(s32[4,1]{0,1:T(1,128)} %param.8) | data formatting | bytes 32 | tf_op args[1]
  9.6 4.3 %all-to-all-done = bf16[8,24,640]{2,1,0:T(8,128)(2,1)S(1)} async-done(((bf16[8,24,640]{2,1,0:T(8,128)(2,1)}), bf16[8,24,640]{2,1,0:T(8,128)(2,1)S(1)}, u32[]{:S(2)}, u32[]{:S(2)}) %all-to-all-start) | async-done | bytes 245792 | tf_op jit(solution)/shard_map/all_to_all | solution.py:324
  13.9 0.9 %unpack.1 = (bf16[136,256]{1,0:T(8,128)(2,1)S(1)}, bf16[136,384]{1,0:T(8,128)(2,1)S(1)}) custom-call(s32[4,1]{1,0:T(4,128)S(1)} %copy.5.offsets_ref, s32[1]{0:T(128)} %copy.9.step_ref, bf16[136,192]{1,0:T(8,128)(2,1)S(1)} %table.1.table_ref, bf16[192,640]{1,0:T(8,128)(2,1)S(1)} %bitcast.8), custom_call_target="tpu_custom_call" | custom-call | tf_op jit(solution)/shard_map/unpack/pallas_call | solution.py:330
  14.8 6.0 %conditional.1 = (bf16[136,384]{1,0:T(8,128)(2,1)}) conditional(s32[]{:T(128)} %clamp.3, bf16[136,384]{1,0:T(8,128)(2,1)S(1)} %get-tuple-element.15, bf16[136,384]{1,0:T(8,128)(2,1)S(1)} %get-tuple-element.15, bf16[136,384]{1,0:T(8,128)(2,1)S(1)} %get-tuple-element.15), branch_computations={%region_0.1_spmd, %region_1.2_spmd, %region_2.3_spmd} | conditional | bytes 417840 | solution.py:342
  14.8 3.7 %collective-permute-start = (bf16[136,384]{1,0:T(8,128)(2,1)S(1)}, bf16[136,384]{1,0:T(8,128)(2,1)}, u32[]{:S(2)}, u32[]{:S(2)}) collective-permute-start(bf16[136,384]{1,0:T(8,128)(2,1)S(1)} %param), channel_id=1, source_target_pairs={{0,3},{1,0},{2,1},{3,2},{4,7},{5,4},{6,5},{7,6},{8,11},{9,8},{10,9... | collective-permute-start | bytes 313352 | tf_op jit(solution)/shard_map/cond/branch_0_fun/ppermute | solution.py:340
  18.5 2.3 %collective-permute-done = bf16[136,384]{1,0:T(8,128)(2,1)} collective-permute-done((bf16[136,384]{1,0:T(8,128)(2,1)S(1)}, bf16[136,384]{1,0:T(8,128)(2,1)}, u32[]{:S(2)}, u32[]{:S(2)}) %collective-permute-start) | collective-permute-done | bytes 104480 | tf_op jit(solution)/shard_map/cond/branch_0_fun/ppermute | solution.py:340
  20.8 9.7 %cost_volume.1 = bf16[128,128,128]{2,1,0:T(8,128)(2,1)} custom-call(bf16[136,256]{1,0:T(8,128)(2,1)S(1)} %get-tuple-element.14.ref_ref, bf16[136,384]{1,0:T(8,128)(2,1)} %get-tuple-element.16.mate_ref), custom_call_target="tpu_custom_call" | custom-call | tf_op jit(solution)/shard_map/cost_volume/pallas_call | solution.py:204
Async XLA Ops:
  2.0 11.9 %all-to-all-start = ((bf16[8,24,640]{2,1,0:T(8,128)(2,1)}), bf16[8,24,640]{2,1,0:T(8,128)(2,1)S(1)}, u32[]{:S(2)}, u32[]{:S(2)}) async-start(bf16[8,24,640]{2,1,0:T(8,128)(2,1)} %pack.1), calls=%async_computation | async-start | bytes 491520 | tf_op jit(solution)/shard_map/all_to_all | solution.py:324
  7.8 0.7 %copy-start = (s32[1024]{0:T(1024)S(1)}, s32[1024]{0:T(1024)}, u32[]{:S(2)}) copy-start(s32[1024]{0:T(1024)} %param.10) | copy-start | bytes 12292
  14.8 6.0 %collective-permute-start = (bf16[136,384]{1,0:T(8,128)(2,1)S(1)}, bf16[136,384]{1,0:T(8,128)(2,1)}, u32[]{:S(2)}, u32[]{:S(2)}) collective-permute-start(bf16[136,384]{1,0:T(8,128)(2,1)S(1)} %param), channel_id=1, source_target_pairs={{0,3},{1,0},{2,1},{3,2},{4,7},{5,4},{6,5},{7,6},{8,11},{9,8},{10,9... | collective-permute-start | bytes 313352 | tf_op jit(solution)/shard_map/cond/branch_0_fun/ppermute | solution.py:340

commit v5 on v4

--- a/solution.py
+++ b/solution.py
@@ -21,18 +21,17 @@
 
 
 def box_sums(values, weights):
-    f32, bf16 = jnp.float32, jnp.bfloat16
-    wide = values.astype(f32)
-    square = wide * wide
-    high = square.astype(bf16)
-    low = (square - high.astype(f32)).astype(bf16)
-    total = jnp.dot(values, weights, preferred_element_type=f32)
-    total_sq = jnp.dot(high, weights, preferred_element_type=f32)
-    return total, total_sq + jnp.dot(low, weights, preferred_element_type=f32)
+    bf16 = jnp.bfloat16
+    rows = values.shape[0]
+    square = values * values
+    high = square.astype(bf16).astype(jnp.float32)
+    lines = jnp.concatenate([values, high, square - high], axis=0).astype(bf16)
+    sums = jnp.dot(lines, weights, preferred_element_type=jnp.float32)
+    return sums[:rows], sums[rows : 2 * rows] + sums[2 * rows :]
 
 
 def cost_kernel(ref_ref, mate_ref, out_ref, ref32, mate32, base_a, base_b, lines_a, lines_b, last_a, last_b, sums_a, sums_b, sent, sems,
-                mate_sum, mate_sq, ref_sum, ref_sq, stats):
+                mate_sum, mate_sq, ref_sum, ref_sq, stats, mate_here, mate_sem):
     step = pl.program_id(0)
     rows = ref_ref.shape[0]
     f32, bf16 = jnp.float32, jnp.bfloat16
@@ -80,20 +79,45 @@
 
     @pl.when(step == 0)
     def _():
+        arrival = pltpu.make_async_copy(mate_ref, mate_here, mate_sem)
+        arrival.start()
+
+        def window(ref):
+            x = [ref[i : i + rows - 8, :] for i in range(9)]
+            return ((x[0] + x[1]) + (x[2] + x[3])) + ((x[4] + x[5]) + (x[6] + x[7])) + x[8]
+
+        def inverse(total, total_sq):
+            mean = total / 81.0
+            return lax.rsqrt(jnp.maximum(total_sq / 81.0 - mean * mean, 0.0) + EPSILON)
+
         ref32[:rows] = ref_ref[...].astype(f32)
-        mate32[:rows] = mate_ref[...].astype(f32)
         ref32[rows:] = jnp.zeros((16, 256), f32)
         mate32[rows:] = jnp.zeros((32, 384), f32)
-        k = lax.broadcasted_iota(jnp.int32, (384, 256), 0)
-        c = lax.broadcasted_iota(jnp.int32, (384, 256), 1)
-        total, total_sq = box_sums(mate_ref[...], ((k - c >= 0) & (k - c <= 8)).astype(bf16))
+        k = lax.broadcasted_iota(jnp.int32, (256, 128), 0)
+        gap_ref = jnp.where(k < 128, k, k - 112) - lax.broadcasted_iota(jnp.int32, (256, 128), 1)
+        weights = ((gap_ref >= 0) & (gap_ref <= 8) & ((k < 128) | (k >= 240))).astype(bf16)
+        ref_sum[...], ref_sq[...] = box_sums(ref32[:rows], weights)
+        total = window(ref_sum)
+        stats[4] = total / 81.0
+        stats[5] = inverse(total, window(ref_sq))
+        k = lax.broadcasted_iota(jnp.int32, (256, 256), 0)
+        c = lax.broadcasted_iota(jnp.int32, (256, 256), 1)
+        weights = ((k - c >= 0) & (k - c <= 8)).astype(bf16)
+        k, c = k[:16] + 256, c[:16]
+        beyond = jnp.where((k - c >= 0) & (k - c <= 8), 1.0, 0.0)
+        beyond = jnp.concatenate([beyond, jnp.zeros((112, 256), f32)], axis=0).astype(bf16)
+        weights = jnp.concatenate([weights, beyond], axis=0)
+        same = lax.broadcasted_iota(jnp.int32, (rows, 256), 0) == lax.broadcasted_iota(jnp.int32, (rows, 256), 1)
+        same = same.astype(bf16)
+        arrival.wait()
+        held = mate_here[...].astype(f32)
+        rest = jnp.concatenate([held[rows:], jnp.zeros((120, 256), f32)], axis=0).astype(bf16)
+        mate32[:rows, :256] = held[:rows]
+        mate32[:rows, 256:] = lax.dot_general(same, rest, (((1,), (1,)), ((), ())), preferred_element_type=f32)
+        total, total_sq = box_sums(mate32[:rows], weights)
         for t in range(2):
             mate_sum[t] = total[:, 128 * t : 128 * t + 128]
             mate_sq[t] = total_sq[:, 128 * t : 128 * t + 128]
-        k = lax.broadcasted_iota(jnp.int32, (256, 128), 0)
-        gap_ref = jnp.where(k < 128, k, k - 112) - lax.broadcasted_iota(jnp.int32, (256, 128), 1)
-        weights = ((gap_ref >= 0) & (gap_ref <= 8) & ((k < 128) | (k >= 240))).astype(bf16)
-        ref_sum[...], ref_sq[...] = box_sums(ref_ref[...], weights)
         for base, first in ((base_b, 0), (base_a, 8)):
             block = lines_from(first)
             for s in range(16):
@@ -106,21 +130,10 @@
         for s in range(16):
             skew(base_b, block, s)
 
-        def window(ref):
-            x = [ref[i : i + rows - 8, :] for i in range(9)]
-            return ((x[0] + x[1]) + (x[2] + x[3])) + ((x[4] + x[5]) + (x[6] + x[7])) + x[8]
-
-        def inverse(total, total_sq):
-            mean = total / 81.0
-            return lax.rsqrt(jnp.maximum(total_sq / 81.0 - mean * mean, 0.0) + EPSILON)
-
         for t in range(2):
             total = window(mate_sum.at[t])
             stats[t] = total
             stats[2 + t] = inverse(total, window(mate_sq.at[t])) / 81.0
-        total = window(ref_sum)
-        stats[4] = total / 81.0
-        stats[5] = inverse(total, window(ref_sq))
 
     def copy(block, half, piece):
         size = DISP // PIECES
@@ -205,7 +218,7 @@
         cost_kernel,
         out_shape=jax.ShapeDtypeStruct((DISP, rows - 8, COLS), jnp.bfloat16),
         grid=((rows - 8) // (2 * RB),),
-        in_specs=[vmem, vmem],
+        in_specs=[vmem, pl.BlockSpec(memory_space=pl.ANY)],
         out_specs=pl.BlockSpec(memory_space=pl.ANY),
         scratch_shapes=[
             pltpu.VMEM((rows + 16, 256), f32),
@@ -225,6 +238,8 @@
             pltpu.VMEM((rows, 128), f32),
             pltpu.VMEM((rows, 128), f32),
             pltpu.VMEM((6, rows - 8, 128), f32),
+            pltpu.VMEM(mate_rows.shape, mate_rows.dtype),
+            pltpu.SemaphoreType.DMA,
         ],
         compiler_params=pltpu.CompilerParams(dimension_semantics=("arbitrary",), vmem_limit_bytes=16 << 20),
         name="cost_volume",
@@ -233,6 +248,7 @@
 
 SPAN = COLS + DISP + 8
 EDGE = 4
+PARTS = 4
 SMALL = pltpu.CompilerParams(vmem_limit_bytes=16 << 20)
 REF_FROM = OFF_MAX + DISP - 1
 
@@ -264,15 +280,32 @@
     return wide == lax.broadcasted_iota(jnp.int32, (strips, slots, line), 1)
 
 
-def pack_kernel(map_ref, tiles_ref, out_ref):
+def pack_kernel(map_ref, tiles_ref, out_ref, map_here, tiles_here, out_here, sems):
     strips, slots, width = out_ref.shape
     rows_dev = tiles_ref.shape[0]
-    ids = jnp.broadcast_to(map_ref[pl.ds(lax.axis_index("strip"), 1), :], (strips, rows_dev))
+    map_copy = pltpu.make_async_copy(map_ref, map_here, sems.at[0])
+    tiles_copy = pltpu.make_async_copy(tiles_ref, tiles_here, sems.at[1])
+    map_copy.start()
+    tiles_copy.start()
+    map_copy.wait()
+    ids = jnp.broadcast_to(map_here[pl.ds(lax.axis_index("strip"), 1), :], (strips, rows_dev))
     low = rows_dev * lax.broadcasted_iota(jnp.int32, (strips, rows_dev), 0)
     rank, _ = places(ids, low, rows_dev)
-    pick = jnp.where(spread(rank, slots), 1.0, 0.0).reshape(strips * slots, rows_dev).astype(jnp.bfloat16)
-    rows = jnp.dot(pick, tiles_ref[...], preferred_element_type=jnp.float32)
-    out_ref[...] = rows.astype(jnp.bfloat16).reshape(out_ref.shape)
+    share = strips // PARTS
+    picks = []
+    for part in range(PARTS):
+        pick = jnp.where(spread(rank[part * share : (part + 1) * share], slots), 1.0, 0.0)
+        picks.append(pick.reshape(share * slots, rows_dev).astype(jnp.bfloat16))
+    tiles_copy.wait()
+    copies = []
+    for part in range(PARTS):
+        lines = pl.ds(part * share, share)
+        rows = jnp.dot(picks[part], tiles_here[...], preferred_element_type=jnp.float32)
+        out_here[lines] = rows.astype(jnp.bfloat16).reshape(share, slots, width)
+        copies.append(pltpu.make_async_copy(out_here.at[lines], out_ref.at[lines], sems.at[2 + part]))
+        copies[-1].start()
+    for copy in copies:
+        copy.wait()
 
 
 def table_kernel(table_ref, out_ref):
@@ -306,7 +339,13 @@
     part = start - whole * 128
     block = strip[:, pl.ds(pl.multiple_of(whole * 128, 128), 512)]
     turned = pltpu.roll(block, 512 - part, axis=1)
-    slab_ref[...] = turned[:, :384].astype(jnp.bfloat16)
+    near = lax.broadcasted_iota(jnp.int32, (16, 128), 0)
+    unit = (near == lax.broadcasted_iota(jnp.int32, (16, 128), 1)).astype(jnp.bfloat16)
+    rest = lax.dot_general(
+        unit, turned[:, 256:384].astype(jnp.bfloat16), (((1,), (1,)), ((), ())), preferred_element_type=jnp.float32
+    )
+    rest = jnp.concatenate([rest[:8], jnp.zeros((8, 256 - rows), jnp.float32)], axis=1)
+    slab_ref[...] = jnp.concatenate([turned[:, :256], rest], axis=0).astype(jnp.bfloat16)
 
 
 def shards(images, offsets, pair_step, row_map):
@@ -318,8 +357,19 @@
     rows = rows_dev + 2 * EDGE
     bf16 = jnp.bfloat16
     table = row_map.reshape(strips, rows_dev)
+    anywhere = pl.BlockSpec(memory_space=pl.ANY)
     outgoing = pl.pallas_call(
-        pack_kernel, out_shape=jax.ShapeDtypeStruct((strips, slots, width), bf16), name="pack"
+        pack_kernel,
+        out_shape=jax.ShapeDtypeStruct((strips, slots, width), bf16),
+        in_specs=[anywhere, anywhere],
+        out_specs=anywhere,
+        scratch_shapes=[
+            pltpu.VMEM((strips, rows_dev), jnp.int32),
+            pltpu.VMEM((rows_dev, width), bf16),
+            pltpu.VMEM((strips, slots, width), bf16),
+            pltpu.SemaphoreType.DMA((2 + PARTS,)),
+        ],
+        name="pack",
     )(table, own_tiles)
     arrived = lax.all_to_all(outgoing, "strip", split_axis=0, concat_axis=0, tiled=True)
     select = pl.pallas_call(
@@ -329,7 +379,7 @@
     vmem = pl.BlockSpec(memory_space=pltpu.VMEM)
     ref_rows, slab = pl.pallas_call(
         unpack_kernel,
-        out_shape=(jax.ShapeDtypeStruct((rows, 256), bf16), jax.ShapeDtypeStruct((rows, 384), bf16)),
+        out_shape=(jax.ShapeDtypeStruct((rows, 256), bf16), jax.ShapeDtypeStruct((rows + 8, 256), bf16)),
         in_specs=[smem, smem, vmem, vmem],
         scratch_shapes=[pltpu.VMEM((rows, 768), jnp.float32)],
         compiler_params=SMALL,

time: 30.8 us -> 30.8 us (level); the launches traced: 30.5 us -> 30.8 us
  waiting for transfers between devices: 6.64 us -> 9.02 us
  starting transfers between devices: 8.83 us -> 6.76 us
    ppermute x1, waiting for transfers between devices: 2.3 us -> 4.68 us  [sent_by(): lax.ppermute(rows_out, 'view', [(i, (i - step) % views) for i in range(vi...]
    ppermute x1, starting transfers between devices: 3.66 us -> 1.58 us  [sent_by(): lax.ppermute(rows_out, 'view', [(i, (i - step) % views) for i in range(vi...]
where the time goes in v5:
time: 30.8 us
  Pallas kernels  12.9 us (42%)
  waiting for transfers between devices  9.02 us (29%)
  starting transfers between devices  6.76 us (22%)
  local copies, waits for them, and re-layouts  1.43 us (5%)
  between operations  0.69 us (2%)
    pallas_call x1, Pallas kernels, cost(): pl.pallas_call(cost_kernel, out_shape=jax.ShapeDtypeStruct((DISP, rows -...  9.75 us
    all_to_all x1, starting transfers between devices, shards(): lax.all_to_all(outgoing, 'strip', split_axis=0, concat_axis=0, tiled=True)  5.18 us
    ppermute x1, waiting for transfers between devices, sent_by(): lax.ppermute(rows_out, 'view', [(i, (i - step) % views) for i in range(vi...  4.68 us
    all_to_all x1, waiting for transfers between devices, shards(): lax.all_to_all(outgoing, 'strip', split_axis=0, concat_axis=0, tiled=True)  4.34 us
    pallas_call x1, Pallas kernels, shards(): pl.pallas_call(pack_kernel, out_shape=jax.ShapeDtypeStruct((strips, slots...  1.86 us
    ppermute x1, starting transfers between devices, sent_by(): lax.ppermute(rows_out, 'view', [(i, (i - step) % views) for i in range(vi...  1.58 us
    unnamed x3, local copies, waits for them, and re-layouts  1.43 us
    pallas_call x1, Pallas kernels, shards(): pl.pallas_call(unpack_kernel, out_shape=(jax.ShapeDtypeStruct((rows, 256)...  1.01 us
  transfers between devices with their start and end apart: 2, of which 2 were waited for; matrix products, arithmetic and copies ran while one was open for 2% of the time, Pallas kernels for 1%

profile of v5, /device:TPU:0, one launch (start us, length us, event | category | flops | bytes accessed | tf_op | source)
XLA Modules:
  0.0 30.8 jit_solution(6850168207052095288)
XLA Ops:
  0.0 1.9 %pack.1 = bf16[8,24,640]{2,1,0:T(8,128)(2,1)} custom-call(s32[8,128]{1,0:T(8,128)} %bitcast.9, bf16[128,640]{1,0:T(8,128)(2,1)} %bitcast.11), custom_call_target="tpu_custom_call" | custom-call | tf_op jit(solution)/shard_map/pack/pallas_call | solution.py:361
  1.9 5.2 %all-to-all-start = ((bf16[8,24,640]{2,1,0:T(8,128)(2,1)}), bf16[8,24,640]{2,1,0:T(8,128)(2,1)S(1)}, u32[]{:S(2)}, u32[]{:S(2)}) async-start(bf16[8,24,640]{2,1,0:T(8,128)(2,1)} %pack.1), calls=%async_computation | async-start | bytes 491520 | tf_op jit(solution)/shard_map/all_to_all | solution.py:374
  7.7 0.0 copy-start
  7.7 0.7 %copy-done = s32[1024]{0:T(1024)S(1)} copy-done((s32[1024]{0:T(1024)S(1)}, s32[1024]{0:T(1024)}, u32[]{:S(2)}) %copy-start) | copy-done | bytes 4120
  8.4 0.3 %table.1.table_ref = bf16[136,192]{1,0:T(8,128)(2,1)S(1)} custom-call(s32[8,128]{1,0:T(8,128)S(1)} %bitcast.10), custom_call_target="tpu_custom_call" | custom-call | tf_op jit(solution)/shard_map/table/pallas_call | solution.py:375
  8.7 0.7 %copy.5.offsets_ref = s32[4,1]{1,0:T(4,128)S(1)} copy(s32[4,1]{0,1:T(1,128)} %param.8) | data formatting | bytes 32 | tf_op args[1]
  9.5 4.3 %all-to-all-done = bf16[8,24,640]{2,1,0:T(8,128)(2,1)S(1)} async-done(((bf16[8,24,640]{2,1,0:T(8,128)(2,1)}), bf16[8,24,640]{2,1,0:T(8,128)(2,1)S(1)}, u32[]{:S(2)}, u32[]{:S(2)}) %all-to-all-start) | async-done | bytes 245792 | tf_op jit(solution)/shard_map/all_to_all | solution.py:374
  13.8 1.0 %unpack.1 = (bf16[136,256]{1,0:T(8,128)(2,1)S(1)}, bf16[144,256]{1,0:T(8,128)(2,1)S(1)}) custom-call(s32[4,1]{1,0:T(4,128)S(1)} %copy.5.offsets_ref, s32[1]{0:T(128)} %copy.9.step_ref, bf16[136,192]{1,0:T(8,128)(2,1)S(1)} %table.1.table_ref, bf16[192,640]{1,0:T(8,128)(2,1)S(1)} %bitcast.8), custom_call_target="tpu_custom_call" | custom-call | tf_op jit(solution)/shard_map/unpack/pallas_call | solution.py:380
  14.8 6.3 %conditional.1 = (bf16[144,256]{1,0:T(8,128)(2,1)}) conditional(s32[]{:T(128)} %clamp.3, bf16[144,256]{1,0:T(8,128)(2,1)S(1)} %get-tuple-element.15, bf16[144,256]{1,0:T(8,128)(2,1)S(1)} %get-tuple-element.15, bf16[144,256]{1,0:T(8,128)(2,1)S(1)} %get-tuple-element.15), branch_computations={%region_0.1_spmd, %region_1.2_spmd, %region_2.3_spmd} | conditional | bytes 294960 | solution.py:392
  14.8 1.6 %collective-permute-start.2 = (bf16[144,256]{1,0:T(8,128)(2,1)S(1)}, bf16[144,256]{1,0:T(8,128)(2,1)}, u32[]{:S(2)}, u32[]{:S(2)}) collective-permute-start(bf16[144,256]{1,0:T(8,128)(2,1)S(1)} %param.2), channel_id=1, source_target_pairs={{0,1},{1,2},{2,3},{3,0},{4,5},{5,6},{6,7},{7,4},{8,9},{9,10},{10,1... | collective-permute-start | bytes 221192 | tf_op jit(solution)/shard_map/cond/branch_2_fun/ppermute | solution.py:390
  16.4 4.7 %collective-permute-done.2 = bf16[144,256]{1,0:T(8,128)(2,1)} collective-permute-done((bf16[144,256]{1,0:T(8,128)(2,1)S(1)}, bf16[144,256]{1,0:T(8,128)(2,1)}, u32[]{:S(2)}, u32[]{:S(2)}) %collective-permute-start.2) | collective-permute-done | bytes 73760 | tf_op jit(solution)/shard_map/cond/branch_2_fun/ppermute | solution.py:390
  21.1 9.7 %cost_volume.1 = bf16[128,128,128]{2,1,0:T(8,128)(2,1)} custom-call(bf16[136,256]{1,0:T(8,128)(2,1)S(1)} %get-tuple-element.14.ref_ref, bf16[144,256]{1,0:T(8,128)(2,1)} %get-tuple-element.16.mate_ref), custom_call_target="tpu_custom_call" | custom-call | tf_op jit(solution)/shard_map/cost_volume/pallas_call | solution.py:217
Async XLA Ops:
  1.9 11.9 %all-to-all-start = ((bf16[8,24,640]{2,1,0:T(8,128)(2,1)}), bf16[8,24,640]{2,1,0:T(8,128)(2,1)S(1)}, u32[]{:S(2)}, u32[]{:S(2)}) async-start(bf16[8,24,640]{2,1,0:T(8,128)(2,1)} %pack.1), calls=%async_computation | async-start | bytes 491520 | tf_op jit(solution)/shard_map/all_to_all | solution.py:374
  7.7 0.7 %copy-start = (s32[1024]{0:T(1024)S(1)}, s32[1024]{0:T(1024)}, u32[]{:S(2)}) copy-start(s32[1024]{0:T(1024)} %param.10) | copy-start | bytes 12292
  14.8 6.3 %collective-permute-start.2 = (bf16[144,256]{1,0:T(8,128)(2,1)S(1)}, bf16[144,256]{1,0:T(8,128)(2,1)}, u32[]{:S(2)}, u32[]{:S(2)}) collective-permute-start(bf16[144,256]{1,0:T(8,128)(2,1)S(1)} %param.2), channel_id=1, source_target_pairs={{0,1},{1,2},{2,3},{3,0},{4,5},{5,6},{6,7},{7,4},{8,9},{9,10},{10,1... | collective-permute-start | bytes 221192 | tf_op jit(solution)/shard_map/cond/branch_2_fun/ppermute | solution.py:390
